TPU v7x, 32 devices: a whole 2x2x4 slice. The times are simulated.
32 devices in a mesh: gx: 16 (over z, y, x), gy: 2 (over core).
Axes of the slice: x: 2, y: 2, z: 4, core: 2. Of those that a mesh axis runs over, the one named last changes fastest.
Arguments:
- observed: float32 [8192, 128], P(('gx', 'gy')), may hold values from -6 to 6
- jacobian: bfloat16 [8192, 64, 128], P(('gx', 'gy'))
- tile_block: int32 [8192], P(('gx', 'gy')), may hold values from 0 to 127
- params: float32 [128, 64], replicated, may hold values from -3 to 3
- damping: float32 [1], replicated, may hold values from 0.05 to 2
Outputs:
- scaled_step: float32 [128, 64], P('gy')
- misfit: float32 [], replicated
All inputs are finite; a program needn't handle non-finite values.
Results may differ from a plain program's by a relative error of at most 0.0031.
Values sent between devices are 32-bit elements; how exact they have to be, the bound alone decides.
No kernel may reach another device: no remote copies, remote signals or barrier semaphores. Data moves between devices by JAX's collectives and lax.ppermute only.
A program may use at most 64 MiB of HBM per device.

v0:
```python
import jax
import jax.numpy as jnp
from jax import lax
from jax.experimental import pallas as pl
from jax.experimental.pallas import tpu as pltpu
from jax.sharding import PartitionSpec as P

NB = 128
STEP_TILES = 64
GROUP = 8
GRAM_UNROLL = 4
GRAD_UNROLL = 4
PACK_UNROLL = 4
PANEL = 8
EXTRA = 8
PLANE = 4


def flipped(value, axes, size):
    return lax.ppermute(value, axes, [(i, size - 1 - i) for i in range(size)])


def xored(value, axis, bit):
    return lax.ppermute(value, axis, [(i, i ^ bit) for i in range(lax.axis_size(axis))])


def plane(value):
    parts = value.reshape(PLANE, value.shape[0] // PLANE, *value.shape[1:])
    total = parts[0]
    for k in range(1, PLANE):
        total = total + xored(parts[k], "gx", k)
    return total


def nt_dot(a, b):
    return lax.dot_general(a, b, (((1,), (1,)), ((), ())), preferred_element_type=jnp.float32)


def gathered(value, index, axis):
    return jnp.take_along_axis(value, index, axis=axis, mode="promise_in_bounds")


def owner_of(c, chunks):
    line = chunks // PLANE
    bits = line.bit_length() - 1
    far = c % line
    swapped = sum(((far >> (bits - 1 - s)) & 1) << s for s in range(bits))
    return (c // line + PLANE * swapped) ^ lax.axis_index("gx")


def first_block(part, c, chunks, per):
    side = lax.axis_index("gy")
    return per * ((side if part == 0 else 1 - side) * chunks + owner_of(c, chunks))


def gram_body(tb, j_ref, par_ref, calc_ref, keep_ref, send_ref, diag_ref, acc, par):
    step = pl.program_id(0)
    blk, vox = j_ref.shape[1:]
    half = blk // 2

    @pl.when(step == 0)
    def _():
        acc[...] = jnp.zeros_like(acc)
        par[...] = par_ref[...].astype(jnp.bfloat16).astype(jnp.float32)

    zero = jnp.zeros((blk, vox), jnp.bfloat16)
    low = lax.broadcasted_iota(jnp.int32, (blk, 2 * blk), 1) < blk

    def group(g, carry):
        base = g * GROUP
        rows = []
        for u in range(0, GROUP, 2):
            left, right = j_ref[base + u], j_ref[base + u + 1]
            lhs = jnp.concatenate([left, right], axis=1)
            rhs = jnp.concatenate(
                [jnp.concatenate([left, zero], axis=1), jnp.concatenate([zero, right], axis=1)], axis=0
            )
            gram = nt_dot(lhs, rhs)
            for v, jac in enumerate((left, right)):
                b = tb[step * STEP_TILES + base + u + v]
                pltpu.store(acc.at[b], acc[b] + gram, mask=low if v == 0 else jnp.logical_not(low))
                spread = gathered(par[...], jnp.full((blk, vox), b, jnp.int32), 1)
                rows.append(jnp.sum(jac.astype(jnp.float32) * spread, axis=0, keepdims=True))
        calc_ref[pl.ds(pl.multiple_of(base, GROUP), GROUP), :] = jnp.concatenate(rows, axis=0)
        return carry

    lax.fori_loop(0, STEP_TILES // GROUP, group, 0, unroll=GRAM_UNROLL)

    @pl.when(step == pl.num_programs(0) - 1)
    def _():
        chunks = keep_ref.shape[0]
        pairs = keep_ref.shape[1] // half
        row = lax.broadcasted_iota(jnp.int32, (half, 2 * blk), 0)
        lane = lax.broadcasted_iota(jnp.int32, (half, 2 * blk), 1) % blk
        use_bot = (lane < half) & (row > lane)
        frow = lax.broadcasted_iota(jnp.int32, (blk, 2 * blk), 0)
        flane = lax.broadcasted_iota(jnp.int32, (blk, 2 * blk), 1) % blk
        on_diag = frow == flane
        for part, ref in enumerate((keep_ref, send_ref)):
            def chunk(c, carry, part=part, ref=ref):
                first = first_block(part, c, chunks, 2 * pairs)
                for p in range(pairs):
                    one, two = acc[first + 2 * p], acc[first + 2 * p + 1]
                    full = jnp.where(low, one, two) + pltpu.roll(jnp.where(low, two, one), blk, 1)
                    bot = pltpu.roll(full[half:], 2 * blk - half, 1)
                    ref[c, p * half : (p + 1) * half, :] = jnp.where(use_bot, bot, full[:half])
                    diag_ref[part, c, p : p + 1, :] = jnp.sum(
                        jnp.where(on_diag, full, 0.0), axis=0, keepdims=True
                    )
                return carry

            lax.fori_loop(0, chunks, chunk, 0, unroll=PACK_UNROLL)


def grad_body(tb, j_ref, calc_ref, obs_ref, mir_ref, diag_ref, keep_ref, send_ref, gacc, mis, mix):
    step = pl.program_id(0)
    blk, vox = j_ref.shape[1:]

    @pl.when(step == 0)
    def _():
        gacc[...] = jnp.zeros_like(gacc)
        mis[...] = jnp.zeros_like(mis)

    back = vox - 1 - lax.broadcasted_iota(jnp.int32, (GROUP, vox), 1)
    up = GROUP - 1 - lax.broadcasted_iota(jnp.int32, (GROUP, vox), 0)
    lane = lax.broadcasted_iota(jnp.int32, (blk, vox), 1)

    def group(g, carry):
        base = pl.multiple_of(g * GROUP, GROUP)
        rows = pl.ds(base, GROUP)
        mirror = mir_ref[pl.ds(pl.multiple_of(STEP_TILES - GROUP - base, GROUP), GROUP), :]
        mirror = gathered(gathered(mirror, back, 1), up, 0)
        resid = 0.5 * (obs_ref[rows, :] + mirror) - calc_ref[rows, :]
        mis[...] += resid * resid
        resid_b = resid.astype(jnp.bfloat16).astype(jnp.float32)
        total = gacc[...]
        for u in range(GROUP):
            b = tb[step * STEP_TILES + base + u]
            grad = jnp.sum(j_ref[base + u].astype(jnp.float32) * resid_b[u : u + 1], axis=1, keepdims=True)
            total = total + jnp.where(lane == b, grad, 0.0)
        gacc[...] = total
        return carry

    lax.fori_loop(0, STEP_TILES // GROUP, group, 0, unroll=GRAD_UNROLL)

    @pl.when(step == pl.num_programs(0) - 1)
    def _():
        chunks = keep_ref.shape[0]
        pairs = diag_ref.shape[2]
        total = jnp.sum(mis[...], axis=0, keepdims=True)
        rest = jnp.zeros((EXTRA - 2 * pairs - 1, vox), jnp.float32)
        wide = jnp.concatenate([gacc[...], jnp.zeros((vox - blk, vox), jnp.float32)], axis=0).T
        by_block = wide + pltpu.roll(wide, blk, 1)
        odd = (lax.broadcasted_iota(jnp.int32, by_block.shape, 0) % 2) == 1
        high = lax.broadcasted_iota(jnp.int32, by_block.shape, 1) >= blk
        spread = jnp.where(odd == high, by_block, 0.0)
        mix[...] = spread
        for part, ref in enumerate((keep_ref, send_ref)):
            def chunk(c, carry, part=part, ref=ref):
                first = first_block(part, c, chunks, 2 * pairs)
                rows = [
                    mix[pl.ds(first + 2 * p, 1), :] + mix[pl.ds(first + 2 * p + 1, 1), :] for p in range(pairs)
                ]
                ref[c] = jnp.concatenate(rows + [diag_ref[part, c], total, rest], axis=0)
                return carry

            lax.fori_loop(0, chunks, chunk, 0, unroll=PACK_UNROLL)


def solve_body(damp, a_ref, b_ref, out_ref, mis_ref):
    x = a_ref[...] + b_ref[...]
    width = x.shape[1]
    blk = width // 2
    half = blk // 2
    tall = blk // 8
    pairs = (x.shape[0] - EXTRA) // half
    ext = x[pairs * half :]
    mis_ref[...] = jnp.broadcast_to(jnp.sum(ext[2 * pairs : 2 * pairs + 1], axis=1, keepdims=True), mis_ref.shape)
    row = lax.broadcasted_iota(jnp.int32, (half, width), 0)
    lane = lax.broadcasted_iota(jnp.int32, (half, width), 1)
    inner = lane % blk
    frow = lax.broadcasted_iota(jnp.int32, (blk, width), 0)
    flane = lax.broadcasted_iota(jnp.int32, (blk, width), 1)
    eye = frow == flane % blk
    scale = damp[0]
    mats = []
    rights = []
    diags = []
    for p in range(pairs):
        t = x[p * half : (p + 1) * half]
        grad = ext[p : p + 1]
        diag = ext[pairs + p : pairs + p + 1]
        tt = jnp.concatenate([t, jnp.zeros((width - half, width), jnp.float32)], axis=0).T
        mt = jnp.where(lane < blk, tt[:half], pltpu.roll(tt[blk : blk + half], blk, 1))
        bt = jnp.where(lane < blk, tt[half:blk], pltpu.roll(tt[blk + half :], blk, 1))
        top = jnp.where((inner < half) & (row > inner), mt, t)
        low = jnp.where(row > inner - half, pltpu.roll(t, half, 1), pltpu.roll(mt, half, 1))
        full = jnp.concatenate([top, jnp.where(inner < half, bt, low)], axis=0)
        full = jnp.where(eye, (diag + scale * diag) + 1.0, full)
        cols = jnp.where(eye, jnp.broadcast_to(grad, (blk, width)), 0.0)
        right = jnp.where(
            flane < blk,
            jnp.sum(jnp.where(flane < blk, cols, 0.0), axis=1, keepdims=True),
            jnp.sum(jnp.where(flane < blk, 0.0, cols), axis=1, keepdims=True),
        )
        mats.append([full[8 * i : 8 * i + 8] for i in range(tall)])
        rights.append([right[8 * i : 8 * i + 8] for i in range(tall)])
        diags.append(diag)
    sub = lax.broadcasted_iota(jnp.int32, (8, width), 0)
    lanes = lax.broadcasted_iota(jnp.int32, (8, width), 1)
    side = lanes - lanes % blk
    for k in range(0, blk, PANEL):
        own = k // 8
        for m, right in zip(mats, rights):
            cols = [[gathered(m[i], side + (k + j), 1) for i in range(tall)] for j in range(PANEL)]
            if k == 0:
                cols.append(right)
            for j in range(PANEL):
                at = (k + j) % 8
                pivot = jnp.broadcast_to(cols[j][own][at : at + 1], (8, width))

                def eliminate(part):
                    prow = jnp.broadcast_to(part[own][at : at + 1], (8, width)) / pivot
                    new = [part[i] - cols[j][i] * prow for i in range(tall)]
                    new[own] = jnp.where(sub == at, prow, new[own])
                    return new

                cols[j + 1 :] = [eliminate(col) for col in cols[j + 1 :]]
                m[:] = eliminate(m)
            if k == 0:
                m[:] = [jnp.where(lanes == side, cols[PANEL][i], m[i]) for i in range(tall)]
    lines = []
    for m, diag in zip(mats, diags):
        line = jnp.zeros((8, width), jnp.float32)
        for i in range(tall):
            line = line + jnp.where(eye[8 * i : 8 * i + 8], gathered(m[i], side, 1), 0.0)
        line = jnp.sum(line, axis=0, keepdims=True) * jnp.sqrt(diag)
        lines += [line, pltpu.roll(line, blk, 1)]
    out = jnp.concatenate(lines, axis=0)
    for c in range(out_ref.shape[0]):
        out_ref[c] = out


def fast(*args):
    return fast_inner(*args)


def fast_inner(observed, jacobian, tile_block, params, damping):
    ngx, ngy = lax.axis_size("gx"), lax.axis_size("gy")
    tiles, blk, vox = jacobian.shape
    per = NB // (ngx * ngy)
    half = blk // 2
    pairs = per // 2
    rows = pairs * half
    moved = flipped(observed, ("gx", "gy"), ngx * ngy)
    bits = ngx.bit_length() - 1
    steps = tiles // STEP_TILES
    payload = jax.ShapeDtypeStruct((ngx, rows, vox), jnp.float32)
    extra = jax.ShapeDtypeStruct((ngx, EXTRA, vox), jnp.float32)
    whole = lambda *shape: pl.BlockSpec(shape, lambda s, *_: (0,) * len(shape))
    jspec = pl.BlockSpec((STEP_TILES, blk, vox), lambda s, *_: (s, 0, 0))
    mspec = pl.BlockSpec((STEP_TILES, vox), lambda s, *_: (steps - 1 - s, 0))
    tspec = pl.BlockSpec((STEP_TILES, vox), lambda s, *_: (s, 0))
    calc, keep, send, diag = pl.pallas_call(
        gram_body,
        out_shape=(
            jax.ShapeDtypeStruct((tiles, vox), jnp.float32),
            payload,
            payload,
            jax.ShapeDtypeStruct((2, ngx, pairs, vox), jnp.float32),
        ),
        grid_spec=pltpu.PrefetchScalarGridSpec(
            num_scalar_prefetch=1,
            grid=(steps,),
            in_specs=[jspec, whole(blk, NB)],
            out_specs=(tspec, whole(ngx, rows, vox), whole(ngx, rows, vox), whole(2, ngx, pairs, vox)),
            scratch_shapes=[pltpu.VMEM((NB, blk, 2 * blk), jnp.float32), pltpu.VMEM((blk, NB), jnp.float32)],
        ),
        name="gram",
    )(tile_block, jacobian, params.T)
    mine = keep + xored(send, "gy", 1)
    tied, mine = lax.optimization_barrier((calc, mine))
    got = plane(mine)
    keep, send = pl.pallas_call(
        grad_body,
        out_shape=(extra, extra),
        grid_spec=pltpu.PrefetchScalarGridSpec(
            num_scalar_prefetch=1,
            grid=(steps,),
            in_specs=[jspec, tspec, tspec, mspec, whole(2, ngx, pairs, vox)],
            out_specs=(whole(ngx, EXTRA, vox), whole(ngx, EXTRA, vox)),
            scratch_shapes=[
                pltpu.VMEM((blk, NB), jnp.float32),
                pltpu.VMEM((GROUP, vox), jnp.float32),
                pltpu.VMEM((NB, vox), jnp.float32),
            ],
        ),
        name="grad",
    )(tile_block, jacobian, tied, observed, moved, diag)
    rest = plane(keep + xored(send, "gy", 1))
    both = jnp.concatenate([got, rest], axis=1)
    mine, got = both, jnp.zeros_like(both)
    for s in range(PLANE.bit_length() - 1, bits):
        n = both.shape[0] // 2
        mine, got = both[:n], xored(both[n:], "gx", 1 << s)
        both = mine + got
    smem = pl.BlockSpec(memory_space=pltpu.SMEM)
    vmem = pl.BlockSpec(memory_space=pltpu.VMEM)
    step, misfit = pl.pallas_call(
        solve_body,
        out_shape=(jax.ShapeDtypeStruct((ngx, per, vox), jnp.float32), jax.ShapeDtypeStruct((8, vox), jnp.float32)),
        in_specs=[smem, vmem, vmem],
        out_specs=(vmem, vmem),
        name="solve",
    )(damping, mine[0], got[0])
    every = lax.all_to_all(step, "gx", 0, 0)
    return every.reshape(ngx * per, vox)[:, :blk], misfit[0, 0] / (tiles * ngx * ngy * vox)


def solve_blocks(system, rhs):
    size = system.shape[1]
    augmented = jnp.concatenate([system, rhs[:, :, None]], axis=2)
    augmented = jnp.transpose(augmented, (1, 2, 0))
    row_ids = jnp.arange(size, dtype=jnp.int32)

    def eliminate(step, current):
        column = step.astype(jnp.int32)
        pivot_row = lax.dynamic_index_in_dim(current, column, 0, keepdims=False)
        pivot = lax.dynamic_index_in_dim(pivot_row, column, 0, keepdims=False)
        pivot_row = pivot_row / pivot[None, :]
        factors = lax.dynamic_index_in_dim(current, column, 1, keepdims=False)
        updated = current - factors[:, None, :] * pivot_row[None, :, :]
        is_pivot = (row_ids == column)[:, None, None]
        return jnp.where(is_pivot, pivot_row[None, :, :], updated)

    final = lax.fori_loop(0, size, eliminate, augmented)
    return jnp.transpose(final[:, size, :], (1, 0))


def general(observed, jacobian, tile_block, params, damping):
    ngx, ngy = lax.axis_size("gx"), lax.axis_size("gy")
    moved = flipped(observed, ("gx", "gy"), ngx * ngy)[::-1, ::-1]
    block_ids = jnp.arange(NB, dtype=jnp.int32)
    onehot = (tile_block[:, None] == block_ids[None, :]).astype(jnp.float32)
    tile_params = jnp.dot(onehot, params, precision=lax.Precision.HIGHEST).astype(jnp.bfloat16)
    calc = jnp.einsum("tpv,tp->tv", jacobian, tile_params, preferred_element_type=jnp.float32)
    resid = 0.5 * (observed + moved) - calc
    local_misfit = jnp.sum(resid * resid)
    resid_b = resid.astype(jnp.bfloat16)
    tile_grad = jnp.einsum("tpv,tv->tp", jacobian, resid_b, preferred_element_type=jnp.float32)
    tile_gram = jnp.einsum("tpv,tqv->tpq", jacobian, jacobian, preferred_element_type=jnp.float32)
    gram = jnp.einsum("tb,tpq->bpq", onehot, tile_gram, precision=lax.Precision.HIGHEST)
    grad = jnp.dot(onehot.T, tile_grad, precision=lax.Precision.HIGHEST)
    owned = NB // ngy
    gram, grad, total = lax.psum((gram, grad, local_misfit), ("gx", "gy"))
    first = lax.axis_index("gy") * owned
    gram = lax.dynamic_slice_in_dim(gram, first, owned, 0)
    grad = lax.dynamic_slice_in_dim(grad, first, owned, 0)
    diagonal = jnp.diagonal(gram, axis1=1, axis2=2)
    eye = jnp.eye(gram.shape[1], dtype=jnp.float32)
    system = gram + damping[0] * diagonal[:, :, None] * eye[None] + eye[None]
    delta = solve_blocks(system, grad)
    return delta * jnp.sqrt(diagonal), total / (observed.size * ngx * ngy)


def solution(mesh):
    ngx, ngy = mesh.shape["gx"], mesh.shape["gy"]
    quick = ngy == 2 and ngx > PLANE and ngx & (ngx - 1) == 0 and NB % (2 * ngx * ngy) == 0
    return jax.shard_map(
        fast if quick else general,
        mesh=mesh,
        in_specs=(P(("gx", "gy"), None), P(("gx", "gy"), None, None), P(("gx", "gy")), P(), P()),
        out_specs=(P("gy", None), P()),
        check_vma=False,
    )
```

profile of v0, /device:TPU:0, one launch (start us, length us, event | category | flops | bytes accessed | tf_op | source)
XLA Modules:
  0.0 75.0 jit_solution(13246864920646491441)
XLA Ops:
  0.6 0.0 copy-start
  0.6 9.6 %gram.1 = (f32[256,128]{1,0:T(8,128)}, f32[16,64,128]{2,1,0:T(8,128)}, f32[16,64,128]{2,1,0:T(8,128)}, f32[2,16,2,128]{3,2,1,0:T(2,128)}) custom-call(s32[256]{0:T(256)} %tb.3, bf16[256,64,128]{2,1,0:T(8,128)(2,1)} %j_ref.3, f32[64,128]{1,0:T(8,128)} %bitcast.9), custom_call_target="tpu_custom_call" | custom-call | tf_op jit(solution)/shard_map/gram/pallas_call | solution.py:264
  10.3 0.5 collective-permute-start
  10.8 0.0 copy-done
  10.8 6.6 %collective-permute-start.4 = (f32[256,128]{1,0:T(8,128)S(1)}, f32[256,128]{1,0:T(8,128)S(1)}, u32[]{:S(2)}, u32[]{:S(2)}) collective-permute-start(f32[256,128]{1,0:T(8,128)S(1)} %copy-done), channel_id=1, source_target_pairs={{0,31},{1,30},{2,29},{3,28},{4,27},{5,26},{6,25},{7,24},{8,23},{9,... | collective-permute-start | bytes 393224 | tf_op jit(solution)/shard_map/ppermute | solution.py:20
  17.3 0.0 collective-permute-done
  17.4 1.1 %add.27 = f32[16,64,128]{2,1,0:T(8,128)S(1)} add(f32[16,64,128]{2,1,0:T(8,128)} %get-tuple-element.13, f32[16,64,128]{2,1,0:T(8,128)S(1)} %collective-permute-done) | non-fusion elementwise | flops 131072 | bytes 1572864 | tf_op jit(solution)/shard_map/add | solution.py:281
  18.5 2.8 %collective-permute-done.4.mir_ref = f32[256,128]{1,0:T(8,128)S(1)} collective-permute-done((f32[256,128]{1,0:T(8,128)S(1)}, f32[256,128]{1,0:T(8,128)S(1)}, u32[]{:S(2)}, u32[]{:S(2)}) %collective-permute-start.4) | collective-permute-done | bytes 131104 | tf_op jit(solution)/shard_map/ppermute | solution.py:20
  21.2 0.0 copy-start.1
  21.2 0.6 copy-done.1
  21.9 8.5 %grad.1 = (f32[16,8,128]{2,1,0:T(8,128)}, f32[16,8,128]{2,1,0:T(8,128)}) custom-call(s32[256]{0:T(256)} %tb.3, bf16[256,64,128]{2,1,0:T(8,128)(2,1)} %j_ref.3, f32[256,128]{1,0:T(8,128)} %get-tuple-element.16.calc_ref, f32[256,128]{1,0:T(8,128)} %obs_ref.1, f32[256,128]{1,0:T(8,128)} %copy-done.1, f32[2,16,2,128]{3,2,1,0:T(2,128)} %get-tuple-element.17.diag_ref), custom_call_target="tpu_custom_call" | custom-call | tf_op jit(solution)/shard_map/grad/pallas_call | solution.py:284
  30.4 0.1 collective-permute-start.5
  30.5 1.4 %collective-permute-done.5 = f32[16,8,128]{2,1,0:T(8,128)S(1)} collective-permute-done((f32[16,8,128]{2,1,0:T(8,128)}, f32[16,8,128]{2,1,0:T(8,128)S(1)}, u32[]{:S(2)}, u32[]{:S(2)}) %collective-permute-start.5) | collective-permute-done | bytes 65568 | tf_op jit(solution)/shard_map/ppermute | solution.py:24
  31.8 0.9 %add.31 = f32[16,8,128]{2,1,0:T(8,128)S(1)} add(f32[16,8,128]{2,1,0:T(8,128)} %get-tuple-element.18, f32[16,8,128]{2,1,0:T(8,128)S(1)} %collective-permute-done.5) | non-fusion elementwise | flops 16384 | bytes 196608 | tf_op jit(solution)/shard_map/add | solution.py:300
  32.7 1.1 %collective-permute-start.6 = (f32[4,8,128]{2,1,0:T(8,128)S(1)}, f32[4,8,128]{2,1,0:T(8,128)S(1)}, u32[]{:S(2)}, u32[]{:S(2)}) collective-permute-start(f32[4,8,128]{2,1,0:T(8,128)S(1)} %get-tuple-element.27), channel_id=1, source_target_pairs={{0,2},{2,0},{4,6},{6,4},{8,10},{10,8},{12,14},{14,12},{16,18},{18,... | collective-permute-start | bytes 49160 | tf_op jit(solution)/shard_map/ppermute | solution.py:24
  33.8 1.5 %collective-permute-start.7 = (f32[4,8,128]{2,1,0:T(8,128)S(1)}, f32[4,8,128]{2,1,0:T(8,128)S(1)}, u32[]{:S(2)}, u32[]{:S(2)}) collective-permute-start(f32[4,8,128]{2,1,0:T(8,128)S(1)} %get-tuple-element.29), channel_id=1, source_target_pairs={{0,4},{2,6},{4,0},{6,2},{8,12},{10,14},{12,8},{14,10},{16,20},{18,... | collective-permute-start | bytes 49160 | tf_op jit(solution)/shard_map/ppermute | solution.py:24
  35.3 0.9 %collective-permute-start.8 = (f32[4,8,128]{2,1,0:T(8,128)S(1)}, f32[4,8,128]{2,1,0:T(8,128)S(1)}, u32[]{:S(2)}, u32[]{:S(2)}) collective-permute-start(f32[4,8,128]{2,1,0:T(8,128)S(1)} %get-tuple-element.28), channel_id=1, source_target_pairs={{0,6},{2,4},{4,2},{6,0},{8,14},{10,12},{12,10},{14,8},{16,22},{18,... | collective-permute-start | bytes 49160 | tf_op jit(solution)/shard_map/ppermute | solution.py:24
  36.3 1.1 %collective-permute-start.1 = (f32[4,64,128]{2,1,0:T(8,128)S(1)}, f32[4,64,128]{2,1,0:T(8,128)S(1)}, u32[]{:S(2)}, u32[]{:S(2)}) collective-permute-start(f32[4,64,128]{2,1,0:T(8,128)S(1)} %get-tuple-element.22), channel_id=1, source_target_pairs={{0,2},{2,0},{4,6},{6,4},{8,10},{10,8},{12,14},{14,12},{16,18},{18,... | collective-permute-start | bytes 393224 | tf_op jit(solution)/shard_map/ppermute | solution.py:24
  37.4 1.5 %collective-permute-start.2 = (f32[4,64,128]{2,1,0:T(8,128)S(1)}, f32[4,64,128]{2,1,0:T(8,128)S(1)}, u32[]{:S(2)}, u32[]{:S(2)}) collective-permute-start(f32[4,64,128]{2,1,0:T(8,128)S(1)} %get-tuple-element.24), channel_id=1, source_target_pairs={{0,4},{2,6},{4,0},{6,2},{8,12},{10,14},{12,8},{14,10},{16,20},{18,... | collective-permute-start | bytes 393224 | tf_op jit(solution)/shard_map/ppermute | solution.py:24
  38.9 0.0 collective-permute-done.6
  38.9 0.9 %collective-permute-start.3 = (f32[4,64,128]{2,1,0:T(8,128)S(1)}, f32[4,64,128]{2,1,0:T(8,128)S(1)}, u32[]{:S(2)}, u32[]{:S(2)}) collective-permute-start(f32[4,64,128]{2,1,0:T(8,128)S(1)} %get-tuple-element.23), channel_id=1, source_target_pairs={{0,6},{2,4},{4,2},{6,0},{8,14},{10,12},{12,10},{14,8},{16,22},{18,... | collective-permute-start | bytes 393224 | tf_op jit(solution)/shard_map/ppermute | solution.py:24
  39.8 0.0 collective-permute-done.7
  39.8 0.3 collective-permute-done.8
  40.1 2.1 %collective-permute-done.1 = f32[4,64,128]{2,1,0:T(8,128)S(1)} collective-permute-done((f32[4,64,128]{2,1,0:T(8,128)S(1)}, f32[4,64,128]{2,1,0:T(8,128)S(1)}, u32[]{:S(2)}, u32[]{:S(2)}) %collective-permute-start.1) | collective-permute-done | bytes 131104 | tf_op jit(solution)/shard_map/ppermute | solution.py:24
  42.2 2.9 %collective-permute-done.2 = f32[4,64,128]{2,1,0:T(8,128)S(1)} collective-permute-done((f32[4,64,128]{2,1,0:T(8,128)S(1)}, f32[4,64,128]{2,1,0:T(8,128)S(1)}, u32[]{:S(2)}, u32[]{:S(2)}) %collective-permute-start.2) | collective-permute-done | bytes 131104 | tf_op jit(solution)/shard_map/ppermute | solution.py:24
  45.2 0.0 collective-permute-done.3
  45.2 2.6 %collective-permute-start.9 = (f32[2,72,128]{2,1,0:T(8,128)S(1)}, f32[2,72,128]{2,1,0:T(8,128)S(1)}, u32[]{:S(2)}, u32[]{:S(2)}) collective-permute-start(f32[2,72,128]{2,1,0:T(8,128)S(1)} %pad_maximum_fusion), channel_id=1, source_target_pairs={{0,8},{2,10},{4,12},{6,14},{8,0},{10,2},{12,4},{14,6},{16,24},{18,... | collective-permute-start | bytes 221192 | tf_op jit(solution)/shard_map/ppermute | solution.py:24
  47.8 2.3 %collective-permute-done.9 = f32[2,72,128]{2,1,0:T(8,128)S(1)} collective-permute-done((f32[2,72,128]{2,1,0:T(8,128)S(1)}, f32[2,72,128]{2,1,0:T(8,128)S(1)}, u32[]{:S(2)}, u32[]{:S(2)}) %collective-permute-start.9) | collective-permute-done | bytes 73760 | tf_op jit(solution)/shard_map/ppermute | solution.py:24
  50.1 0.6 fusion.5
  50.7 3.0 %collective-permute-start.10 = (f32[1,72,128]{2,1,0:T(8,128)S(1)}, f32[1,72,128]{2,1,0:T(8,128)S(1)}, u32[]{:S(2)}, u32[]{:S(2)}) collective-permute-start(f32[1,72,128]{2,1,0:T(8,128)S(1)} %get-tuple-element.25), channel_id=1, source_target_pairs={{0,16},{2,18},{4,20},{6,22},{8,24},{10,26},{12,28},{14,30},{16,0},... | collective-permute-start | bytes 110600 | tf_op jit(solution)/shard_map/ppermute | solution.py:24
  54.4 1.3 %collective-permute-done.10 = f32[1,72,128]{2,1,0:T(8,128)S(1)} collective-permute-done((f32[1,72,128]{2,1,0:T(8,128)S(1)}, f32[1,72,128]{2,1,0:T(8,128)S(1)}, u32[]{:S(2)}, u32[]{:S(2)}) %collective-permute-start.10) | collective-permute-done | bytes 36896 | tf_op jit(solution)/shard_map/ppermute | solution.py:24
  55.7 0.0 copy-start.2
  55.7 0.6 copy-done.2
  56.3 4.2 %solve.1 = (f32[16,4,128]{2,1,0:T(4,128)}, f32[8,128]{1,0:T(8,128)}) custom-call(f32[1]{0:T(128)S(6)} %copy.8.damp, f32[72,128]{1,0:T(8,128)} %get-tuple-element.26.a_ref, f32[72,128]{1,0:T(8,128)} %bitcast.8), custom_call_target="tpu_custom_call" | custom-call | tf_op jit(solution)/shard_map/solve/pallas_call | solution.py:309
  60.5 5.3 %all-to-all-start = ((f32[16,4,128]{2,1,0:T(4,128)}), f32[16,4,128]{2,1,0:T(4,128)S(1)}, u32[]{:S(2)}, u32[]{:S(2)}) async-start(f32[16,4,128]{2,1,0:T(4,128)} %get-tuple-element.20), calls=%async_computation | async-start | bytes 65536 | tf_op jit(solution)/shard_map/all_to_all | solution.py:316
  65.9 1.2 %slice.63 = f32[1,1]{1,0:T(1,128)} slice(f32[8,128]{1,0:T(8,128)} %get-tuple-element.21), slice={[0:1], [0:1]} | slice | bytes 8 | tf_op jit(solution)/shard_map/slice | solution.py:317
  67.7 5.6 %all-to-all-done = f32[16,4,128]{2,1,0:T(4,128)S(1)} async-done(((f32[16,4,128]{2,1,0:T(4,128)}), f32[16,4,128]{2,1,0:T(4,128)S(1)}, u32[]{:S(2)}, u32[]{:S(2)}) %all-to-all-start) | async-done | bytes 32800 | tf_op jit(solution)/shard_map/all_to_all | solution.py:316
  73.3 0.6 copy.9
  (6 shorter events, 0.1 us)
Async XLA Ops:
  0.6 10.1 %copy-start = (f32[256,128]{1,0:T(8,128)S(1)}, f32[256,128]{1,0:T(8,128)}, u32[]{:S(2)}) copy-start(f32[256,128]{1,0:T(8,128)} %obs_ref.1) | copy-start | bytes 393220
  10.3 7.1 %collective-permute-start = (f32[16,64,128]{2,1,0:T(8,128)}, f32[16,64,128]{2,1,0:T(8,128)S(1)}, u32[]{:S(2)}, u32[]{:S(2)}) collective-permute-start(f32[16,64,128]{2,1,0:T(8,128)} %get-tuple-element.14), channel_id=1, source_target_pairs={{0,1},{1,0},{2,3},{3,2},{4,5},{5,4},{6,7},{7,6},{8,9},{9,8},{10,11... | collective-permute-start | bytes 1572872 | tf_op jit(solution)/shard_map/ppermute | solution.py:24
  10.8 10.5 %collective-permute-start.4 = (f32[256,128]{1,0:T(8,128)S(1)}, f32[256,128]{1,0:T(8,128)S(1)}, u32[]{:S(2)}, u32[]{:S(2)}) collective-permute-start(f32[256,128]{1,0:T(8,128)S(1)} %copy-done), channel_id=1, source_target_pairs={{0,31},{1,30},{2,29},{3,28},{4,27},{5,26},{6,25},{7,24},{8,23},{9,... | collective-permute-start | bytes 393224 | tf_op jit(solution)/shard_map/ppermute | solution.py:20
  21.2 0.6 copy-start.1
  30.4 1.5 %collective-permute-start.5 = (f32[16,8,128]{2,1,0:T(8,128)}, f32[16,8,128]{2,1,0:T(8,128)S(1)}, u32[]{:S(2)}, u32[]{:S(2)}) collective-permute-start(f32[16,8,128]{2,1,0:T(8,128)} %get-tuple-element.19), channel_id=1, source_target_pairs={{0,1},{1,0},{2,3},{3,2},{4,5},{5,4},{6,7},{7,6},{8,9},{9,8},{10,11... | collective-permute-start | bytes 196616 | tf_op jit(solution)/shard_map/ppermute | solution.py:24
  32.7 6.2 %collective-permute-start.6 = (f32[4,8,128]{2,1,0:T(8,128)S(1)}, f32[4,8,128]{2,1,0:T(8,128)S(1)}, u32[]{:S(2)}, u32[]{:S(2)}) collective-permute-start(f32[4,8,128]{2,1,0:T(8,128)S(1)} %get-tuple-element.27), channel_id=1, source_target_pairs={{0,2},{2,0},{4,6},{6,4},{8,10},{10,8},{12,14},{14,12},{16,18},{18,... | collective-permute-start | bytes 49160 | tf_op jit(solution)/shard_map/ppermute | solution.py:24
  33.8 6.0 %collective-permute-start.7 = (f32[4,8,128]{2,1,0:T(8,128)S(1)}, f32[4,8,128]{2,1,0:T(8,128)S(1)}, u32[]{:S(2)}, u32[]{:S(2)}) collective-permute-start(f32[4,8,128]{2,1,0:T(8,128)S(1)} %get-tuple-element.29), channel_id=1, source_target_pairs={{0,4},{2,6},{4,0},{6,2},{8,12},{10,14},{12,8},{14,10},{16,20},{18,... | collective-permute-start | bytes 49160 | tf_op jit(solution)/shard_map/ppermute | solution.py:24
  35.3 4.8 %collective-permute-start.8 = (f32[4,8,128]{2,1,0:T(8,128)S(1)}, f32[4,8,128]{2,1,0:T(8,128)S(1)}, u32[]{:S(2)}, u32[]{:S(2)}) collective-permute-start(f32[4,8,128]{2,1,0:T(8,128)S(1)} %get-tuple-element.28), channel_id=1, source_target_pairs={{0,6},{2,4},{4,2},{6,0},{8,14},{10,12},{12,10},{14,8},{16,22},{18,... | collective-permute-start | bytes 49160 | tf_op jit(solution)/shard_map/ppermute | solution.py:24
  36.3 5.9 %collective-permute-start.1 = (f32[4,64,128]{2,1,0:T(8,128)S(1)}, f32[4,64,128]{2,1,0:T(8,128)S(1)}, u32[]{:S(2)}, u32[]{:S(2)}) collective-permute-start(f32[4,64,128]{2,1,0:T(8,128)S(1)} %get-tuple-element.22), channel_id=1, source_target_pairs={{0,2},{2,0},{4,6},{6,4},{8,10},{10,8},{12,14},{14,12},{16,18},{18,... | collective-permute-start | bytes 393224 | tf_op jit(solution)/shard_map/ppermute | solution.py:24
  37.4 7.8 %collective-permute-start.2 = (f32[4,64,128]{2,1,0:T(8,128)S(1)}, f32[4,64,128]{2,1,0:T(8,128)S(1)}, u32[]{:S(2)}, u32[]{:S(2)}) collective-permute-start(f32[4,64,128]{2,1,0:T(8,128)S(1)} %get-tuple-element.24), channel_id=1, source_target_pairs={{0,4},{2,6},{4,0},{6,2},{8,12},{10,14},{12,8},{14,10},{16,20},{18,... | collective-permute-start | bytes 393224 | tf_op jit(solution)/shard_map/ppermute | solution.py:24
  38.9 6.3 %collective-permute-start.3 = (f32[4,64,128]{2,1,0:T(8,128)S(1)}, f32[4,64,128]{2,1,0:T(8,128)S(1)}, u32[]{:S(2)}, u32[]{:S(2)}) collective-permute-start(f32[4,64,128]{2,1,0:T(8,128)S(1)} %get-tuple-element.23), channel_id=1, source_target_pairs={{0,6},{2,4},{4,2},{6,0},{8,14},{10,12},{12,10},{14,8},{16,22},{18,... | collective-permute-start | bytes 393224 | tf_op jit(solution)/shard_map/ppermute | solution.py:24
  45.2 4.9 %collective-permute-start.9 = (f32[2,72,128]{2,1,0:T(8,128)S(1)}, f32[2,72,128]{2,1,0:T(8,128)S(1)}, u32[]{:S(2)}, u32[]{:S(2)}) collective-permute-start(f32[2,72,128]{2,1,0:T(8,128)S(1)} %pad_maximum_fusion), channel_id=1, source_target_pairs={{0,8},{2,10},{4,12},{6,14},{8,0},{10,2},{12,4},{14,6},{16,24},{18,... | collective-permute-start | bytes 221192 | tf_op jit(solution)/shard_map/ppermute | solution.py:24
  50.7 5.0 %collective-permute-start.10 = (f32[1,72,128]{2,1,0:T(8,128)S(1)}, f32[1,72,128]{2,1,0:T(8,128)S(1)}, u32[]{:S(2)}, u32[]{:S(2)}) collective-permute-start(f32[1,72,128]{2,1,0:T(8,128)S(1)} %get-tuple-element.25), channel_id=1, source_target_pairs={{0,16},{2,18},{4,20},{6,22},{8,24},{10,26},{12,28},{14,30},{16,0},... | collective-permute-start | bytes 110600 | tf_op jit(solution)/shard_map/ppermute | solution.py:24
  55.7 0.6 copy-start.2
  60.5 12.8 %all-to-all-start = ((f32[16,4,128]{2,1,0:T(4,128)}), f32[16,4,128]{2,1,0:T(4,128)S(1)}, u32[]{:S(2)}, u32[]{:S(2)}) async-start(f32[16,4,128]{2,1,0:T(4,128)} %get-tuple-element.20), calls=%async_computation | async-start | bytes 65536 | tf_op jit(solution)/shard_map/all_to_all | solution.py:316
where the time goes:
time: 75.6 us; the launch traced here: 75 us
  starting transfers between devices  25.2 us (33%)
  Pallas kernels  22.3 us (29%)
  waiting for transfers between devices  18.6 us (25%)
  local copies, waits for them, and re-layouts  3.71 us (5%)
  between operations  3.11 us (4%)
  other arithmetic  2.04 us (3%)
    ppermute x10, starting transfers between devices, xored(): lax.ppermute(value, axis, [(i, i ^ bit) for i in range(lax.axis_size(axis...  13.3 us
    ppermute x10, waiting for transfers between devices, xored(): lax.ppermute(value, axis, [(i, i ^ bit) for i in range(lax.axis_size(axis...  10.3 us
    pallas_call x1, Pallas kernels, fast_inner(): pl.pallas_call(gram_body, out_shape=(jax.ShapeDtypeStruct((tiles, vox), j...  9.63 us
    pallas_call x1, Pallas kernels, fast_inner(): pl.pallas_call(grad_body, out_shape=(extra, extra), grid_spec=pltpu.Prefe...  8.49 us
    ppermute x1, starting transfers between devices, flipped(): return lax.ppermute(value, axes, [(i, size - 1 - i) for i in range(size)])  6.58 us
    all_to_all x1, waiting for transfers between devices, fast_inner(): every = lax.all_to_all(step, 'gx', 0, 0)  5.56 us
    all_to_all x1, starting transfers between devices, fast_inner(): every = lax.all_to_all(step, 'gx', 0, 0)  5.35 us
    pallas_call x1, Pallas kernels, fast_inner(): pl.pallas_call(solve_body, out_shape=(jax.ShapeDtypeStruct((ngx, per, vox...  4.22 us
  transfers between devices with their start and end apart: 12, of which 8 were waited for; matrix products, arithmetic and copies ran while one was open for 3% of the time, Pallas kernels for 0%

commit v1 on v0

v1 whole, which is shorter than its diff:
```python
import jax
import jax.numpy as jnp
from jax import lax
from jax.experimental import pallas as pl
from jax.experimental.pallas import tpu as pltpu
from jax.sharding import PartitionSpec as P

NB = 128
J_PARTS = 4
GROUP = 8
GRAM_UNROLL = 4
GRAD_UNROLL = 8
PACK_UNROLL = 4
PANEL = 8
VMEM_LIMIT = 20 << 20
EXTRA = 8
PLANE = 4


def flipped(value, axes, size):
    return lax.ppermute(value, axes, [(i, size - 1 - i) for i in range(size)])


def xored(value, axis, bit):
    return lax.ppermute(value, axis, [(i, i ^ bit) for i in range(lax.axis_size(axis))])


def plane(value):
    parts = value.reshape(PLANE, value.shape[0] // PLANE, *value.shape[1:])
    total = parts[0]
    for k in range(1, PLANE):
        total = total + xored(parts[k], "gx", k)
    return total


def nt_dot(a, b):
    return lax.dot_general(a, b, (((1,), (1,)), ((), ())), preferred_element_type=jnp.float32)


def gathered(value, index, axis):
    return jnp.take_along_axis(value, index, axis=axis, mode="promise_in_bounds")


def owner_of(c, chunks):
    line = chunks // PLANE
    bits = line.bit_length() - 1
    far = c % line
    swapped = sum(((far >> (bits - 1 - s)) & 1) << s for s in range(bits))
    return (c // line + PLANE * swapped) ^ lax.axis_index("gx")


def first_block(part, c, chunks, per):
    side = lax.axis_index("gy")
    return per * ((side if part == 0 else 1 - side) * chunks + owner_of(c, chunks))


def copies(j_ref, jbuf, sems):
    count = sems.shape[0]
    size = jbuf.shape[1] // count
    parts = []
    for c in range(count):
        rows = pl.ds(c * size, size)
        parts.append(pltpu.make_async_copy(j_ref.at[:, rows], jbuf.at[:, rows], sems.at[c]))
        parts[-1].start()
    return parts, size // GROUP


def diagonal_pair(left, right, zero):
    return jnp.concatenate(
        [jnp.concatenate([left, zero], axis=1), jnp.concatenate([zero, right], axis=1)], axis=0
    )


def gram_body(tb, j_ref, par_ref, calc_ref, keep_ref, send_ref, diag_ref, jbuf, acc, par, sems):
    parts, groups = copies(j_ref, jbuf, sems)
    side_tiles, blk, vox = jbuf.shape[1:]
    half = blk // 2
    acc[...] = jnp.zeros_like(acc)
    par[...] = jnp.concatenate([par_ref[...], par_ref[...]], axis=0).T.astype(jnp.bfloat16).astype(jnp.float32)
    zero = jnp.zeros((blk, vox), jnp.bfloat16)
    low = lax.broadcasted_iota(jnp.int32, (blk, 2 * blk), 1) < blk
    high = jnp.logical_not(low)
    grow = lax.broadcasted_iota(jnp.int32, (GROUP, 2 * blk), 0)
    gside = (lax.broadcasted_iota(jnp.int32, (GROUP, 2 * blk), 1) >= blk).astype(jnp.int32)
    slot = grow - (grow & 1) + gside
    fits = grow == slot

    def group(g, carry):
        base = pl.multiple_of(g * GROUP, GROUP)
        for h in range(2):
            rows = jnp.concatenate(
                [par[pl.ds(tb[h * side_tiles + base + u], 1), :] for u in range(GROUP)], axis=0
            )
            rows = jnp.where(fits, rows, 0.0)
            total = jnp.zeros((GROUP, vox), jnp.float32)
            for a in range(0, GROUP, 4):
                lhs = [jnp.where((grow >= a + v) & (grow < a + v + 2), rows, 0.0) for v in (0, 2)]
                lhs = jnp.concatenate(lhs, axis=1).astype(jnp.bfloat16)
                four = jbuf[h, pl.ds(base + a, 4)].reshape(4 * blk, vox)
                total = total + jnp.dot(lhs, four, preferred_element_type=jnp.float32)
            calc_ref[h, pl.ds(base, GROUP), :] = total
        for u in range(GROUP):
            left, right = jbuf[0, base + u], jbuf[1, base + u]
            gram = nt_dot(jnp.concatenate([left, right], axis=1), diagonal_pair(left, right, zero))
            one, two = tb[base + u], tb[side_tiles + base + u]
            low_sum, high_sum = acc[one] + gram, acc[two] + gram
            pltpu.store(acc.at[one], low_sum, mask=low)
            pltpu.store(acc.at[two], high_sum, mask=high)
        return carry

    for c, part in enumerate(parts):
        part.wait()
        lax.fori_loop(c * groups, (c + 1) * groups, group, 0, unroll=GRAM_UNROLL)

    chunks = keep_ref.shape[0]
    pairs = keep_ref.shape[1] // half
    row = lax.broadcasted_iota(jnp.int32, (half, 2 * blk), 0)
    lane = lax.broadcasted_iota(jnp.int32, (half, 2 * blk), 1) % blk
    use_top = ((lane < half) & (row <= lane)) | ((lane >= half) & (lane - half <= row))
    frow = lax.broadcasted_iota(jnp.int32, (blk, 2 * blk), 0)
    flane = lax.broadcasted_iota(jnp.int32, (blk, 2 * blk), 1) % blk
    on_diag = frow == flane
    for part, ref in enumerate((send_ref, keep_ref)):
        def chunk(c, carry, part=1 - part, ref=ref):
            first = first_block(part, c, chunks, 2 * pairs)
            for p in range(pairs):
                one, two = acc[first + 2 * p], acc[first + 2 * p + 1]
                stay, cross = jnp.where(low, one, two), jnp.where(low, two, one)
                ref[c, p * half : (p + 1) * half, :] = jnp.where(use_top, stay[:half], stay[half:]) + pltpu.roll(
                    jnp.where(use_top, cross[:half], cross[half:]), blk, 1
                )
                lines = [jnp.sum(jnp.where(on_diag, v, 0.0), axis=0, keepdims=True) for v in (stay, cross)]
                diag_ref[part, c, p : p + 1, :] = lines[0] + pltpu.roll(lines[1], blk, 1)
            return carry

        lax.fori_loop(0, chunks, chunk, 0, unroll=PACK_UNROLL)


def grad_body(tb_ref, jbuf, calc_ref, obs_ref, mir_ref, diag_ref, keep_ref, send_ref, tg, mix):
    side_tiles, blk, vox = jbuf.shape[1:]
    tb_rows = tb_ref[...]
    back = vox - 1 - lax.broadcasted_iota(jnp.int32, (GROUP, vox), 1)
    up = GROUP - 1 - lax.broadcasted_iota(jnp.int32, (GROUP, vox), 0)
    sub = lax.broadcasted_iota(jnp.int32, (GROUP, vox), 0)
    zero = jnp.zeros((blk, vox), jnp.bfloat16)

    def group(g, mis):
        base = pl.multiple_of(g * GROUP, GROUP)
        rows = pl.ds(base, GROUP)
        resids = []
        for h in range(2):
            mirror = mir_ref[1 - h, pl.ds(pl.multiple_of(side_tiles - GROUP - base, GROUP), GROUP), :]
            mirror = gathered(gathered(mirror, back, 1), up, 0)
            resid = 0.5 * (obs_ref[h, rows, :] + mirror) - calc_ref[h, rows, :]
            mis = mis + resid * resid
            resids.append(resid)
        lhs = jnp.concatenate(resids, axis=1).astype(jnp.bfloat16)
        lines = jnp.zeros((GROUP, vox), jnp.float32)
        for u in range(GROUP):
            grad = nt_dot(lhs, diagonal_pair(jbuf[0, base + u], jbuf[1, base + u], zero))
            lines = jnp.where(sub == u, grad, lines)
        tg[rows, :] = lines
        return mis

    mis = lax.fori_loop(0, side_tiles // GROUP, group, jnp.zeros((GROUP, vox), jnp.float32), unroll=GRAD_UNROLL)

    chunks = keep_ref.shape[0]
    pairs = diag_ref.shape[2]
    total = jnp.sum(mis, axis=0, keepdims=True)
    rest = jnp.zeros((EXTRA - 2 * pairs - 1, vox), jnp.float32)
    block = lax.broadcasted_iota(jnp.int32, (NB, side_tiles), 0)
    sums = [
        jnp.dot(
            (block == tb_row).astype(jnp.float32),
            tg[...],
            precision=lax.Precision.HIGHEST,
            preferred_element_type=jnp.float32,
        )
        for tb_row in (tb_rows[0:1], tb_rows[1:2])
    ]
    high = lax.broadcasted_iota(jnp.int32, sums[0].shape, 1) >= blk
    odd = (lax.broadcasted_iota(jnp.int32, sums[0].shape, 0) % 2) == 1
    own = jnp.where(high, sums[1], sums[0])
    mix[...] = jnp.where(odd == high, own + pltpu.roll(own, blk, 1), 0.0)
    for part, ref in enumerate((keep_ref, send_ref)):
        def chunk(c, carry, part=part, ref=ref):
            first = first_block(part, c, chunks, 2 * pairs)
            rows = [mix[pl.ds(first + 2 * p, 1), :] + mix[pl.ds(first + 2 * p + 1, 1), :] for p in range(pairs)]
            ref[c] = jnp.concatenate(rows + [diag_ref[part, c], total, rest], axis=0)
            return carry

        lax.fori_loop(0, chunks, chunk, 0, unroll=PACK_UNROLL)


def solve_body(damp, a_ref, b_ref, out_ref, mis_ref):
    x = a_ref[0] + b_ref[0]
    width = x.shape[1]
    blk = width // 2
    half = blk // 2
    tall = blk // 8
    pairs = (x.shape[0] - EXTRA) // half
    ext = x[pairs * half :]
    mis_ref[...] = jnp.broadcast_to(jnp.sum(ext[2 * pairs : 2 * pairs + 1], axis=1, keepdims=True), mis_ref.shape)
    row = lax.broadcasted_iota(jnp.int32, (half, width), 0)
    lane = lax.broadcasted_iota(jnp.int32, (half, width), 1)
    inner = lane % blk
    frow = lax.broadcasted_iota(jnp.int32, (blk, width), 0)
    flane = lax.broadcasted_iota(jnp.int32, (blk, width), 1)
    eye = frow == flane % blk
    scale = damp[0]
    mats = []
    rights = []
    diags = []
    for p in range(pairs):
        t = x[p * half : (p + 1) * half]
        grad = ext[p : p + 1]
        diag = ext[pairs + p : pairs + p + 1]
        tt = jnp.concatenate([t, jnp.zeros((width - half, width), jnp.float32)], axis=0).T
        mt = jnp.where(lane < blk, tt[:half], pltpu.roll(tt[blk : blk + half], blk, 1))
        bt = jnp.where(lane < blk, tt[half:blk], pltpu.roll(tt[blk + half :], blk, 1))
        top = jnp.where(
            inner < half,
            jnp.where(row <= inner, t, mt),
            jnp.where(inner - half <= row, t, pltpu.roll(mt, half, 1)),
        )
        bot = jnp.where(
            inner < half,
            jnp.where(row > inner, t, bt),
            jnp.where(inner - half > row, t, pltpu.roll(bt, half, 1)),
        )
        full = jnp.concatenate([top, bot], axis=0)
        full = jnp.where(eye, (diag + scale * diag) + 1.0, full)
        cols = jnp.where(eye, jnp.broadcast_to(grad, (blk, width)), 0.0)
        right = jnp.where(
            flane < blk,
            jnp.sum(jnp.where(flane < blk, cols, 0.0), axis=1, keepdims=True),
            jnp.sum(jnp.where(flane < blk, 0.0, cols), axis=1, keepdims=True),
        )
        mats.append([full[8 * i : 8 * i + 8] for i in range(tall)])
        rights.append([right[8 * i : 8 * i + 8] for i in range(tall)])
        diags.append(diag)
    sub = lax.broadcasted_iota(jnp.int32, (8, width), 0)
    lanes = lax.broadcasted_iota(jnp.int32, (8, width), 1)
    side = lanes - lanes % blk
    for k in range(0, blk, PANEL):
        own = k // 8
        for m, right in zip(mats, rights):
            cols = [[gathered(m[i], side + (k + j), 1) for i in range(tall)] for j in range(PANEL)]
            if k == 0:
                cols.append(right)
            for j in range(PANEL):
                at = (k + j) % 8
                pivot = jnp.broadcast_to(cols[j][own][at : at + 1], (8, width))

                def eliminate(part):
                    prow = jnp.broadcast_to(part[own][at : at + 1], (8, width)) / pivot
                    new = [part[i] - cols[j][i] * prow for i in range(tall)]
                    new[own] = jnp.where(sub == at, prow, new[own])
                    return new

                cols[j + 1 :] = [eliminate(col) for col in cols[j + 1 :]]
                m[:] = eliminate(m)
            if k == 0:
                m[:] = [jnp.where(lanes == side, cols[PANEL][i], m[i]) for i in range(tall)]
    lines = []
    for m, diag in zip(mats, diags):
        line = jnp.zeros((8, width), jnp.float32)
        for i in range(tall):
            line = line + jnp.where(eye[8 * i : 8 * i + 8], gathered(m[i], side, 1), 0.0)
        line = jnp.sum(line, axis=0, keepdims=True) * jnp.sqrt(diag)
        lines += [line, pltpu.roll(line, blk, 1)]
    out = jnp.concatenate(lines, axis=0)
    for c in range(out_ref.shape[0]):
        out_ref[c] = out


def fast(*args):
    return fast_inner(*args)


def fast_inner(observed, jacobian, tile_block, params, damping):
    ngx, ngy = lax.axis_size("gx"), lax.axis_size("gy")
    tiles, blk, vox = jacobian.shape
    per = NB // (ngx * ngy)
    half = blk // 2
    pairs = per // 2
    rows = pairs * half
    moved = flipped(observed, ("gx", "gy"), ngx * ngy)
    bits = ngx.bit_length() - 1
    side_tiles = tiles // 2
    local = lambda value: pltpu.with_memory_space_constraint(value, pltpu.VMEM)
    limit = pltpu.CompilerParams(vmem_limit_bytes=VMEM_LIMIT)
    halved = lambda value: value.reshape(2, side_tiles, *value.shape[1:])
    payload = pltpu.VMEM((ngx, rows, vox), jnp.float32)
    extra = pltpu.VMEM((ngx, EXTRA, vox), jnp.float32)
    smem = pl.BlockSpec(memory_space=pltpu.SMEM)
    vmem = pl.BlockSpec(memory_space=pltpu.VMEM)
    hbm = pl.BlockSpec(memory_space=pl.ANY)
    far = lambda value: pltpu.with_memory_space_constraint(value, pltpu.HBM)
    calc, keep, send, diag, staged = pl.pallas_call(
        gram_body,
        out_shape=(
            pltpu.VMEM((2, side_tiles, vox), jnp.float32),
            payload,
            payload,
            pltpu.VMEM((2, ngx, pairs, vox), jnp.float32),
            pltpu.VMEM((2, side_tiles, blk, vox), jnp.bfloat16),
        ),
        in_specs=[smem, hbm, vmem],
        out_specs=(vmem, vmem, vmem, vmem, vmem),
        scratch_shapes=[
            pltpu.VMEM((NB, blk, 2 * blk), jnp.float32),
            pltpu.VMEM((NB, 2 * blk), jnp.float32),
            pltpu.SemaphoreType.DMA((J_PARTS,)),
        ],
        compiler_params=limit,
        name="gram",
    )(far(tile_block), far(halved(jacobian)), far(params.T))
    mine = keep + xored(send, "gy", 1)
    tied, mine = lax.optimization_barrier((calc, mine))
    got = plane(mine)
    keep, send = pl.pallas_call(
        grad_body,
        out_shape=(extra, extra),
        in_specs=[vmem] * 6,
        out_specs=(vmem, vmem),
        scratch_shapes=[pltpu.VMEM((side_tiles, vox), jnp.float32), pltpu.VMEM((NB, vox), jnp.float32)],
        compiler_params=limit,
        name="grad",
    )(halved(tile_block), local(staged), local(tied), halved(observed), local(halved(moved)), local(diag))
    rest = plane(keep + xored(send, "gy", 1))
    both = jnp.concatenate([got, rest], axis=1)
    mine, got = both, jnp.zeros_like(both)
    for s in range(PLANE.bit_length() - 1, bits):
        n = both.shape[0] // 2
        mine, got = both[:n], xored(both[n:], "gx", 1 << s)
        both = mine + got
    step, misfit = pl.pallas_call(
        solve_body,
        out_shape=(jax.ShapeDtypeStruct((ngx, per, vox), jnp.float32), jax.ShapeDtypeStruct((8, vox), jnp.float32)),
        in_specs=[smem, vmem, vmem],
        out_specs=(vmem, vmem),
        compiler_params=limit,
        name="solve",
    )(damping, local(mine), local(got))
    every = lax.all_to_all(step, "gx", 0, 0)
    return every.reshape(ngx * per, vox)[:, :blk], misfit[0, 0] / (tiles * ngx * ngy * vox)


def solve_blocks(system, rhs):
    size = system.shape[1]
    augmented = jnp.concatenate([system, rhs[:, :, None]], axis=2)
    augmented = jnp.transpose(augmented, (1, 2, 0))
    row_ids = jnp.arange(size, dtype=jnp.int32)

    def eliminate(step, current):
        column = step.astype(jnp.int32)
        pivot_row = lax.dynamic_index_in_dim(current, column, 0, keepdims=False)
        pivot = lax.dynamic_index_in_dim(pivot_row, column, 0, keepdims=False)
        pivot_row = pivot_row / pivot[None, :]
        factors = lax.dynamic_index_in_dim(current, column, 1, keepdims=False)
        updated = current - factors[:, None, :] * pivot_row[None, :, :]
        is_pivot = (row_ids == column)[:, None, None]
        return jnp.where(is_pivot, pivot_row[None, :, :], updated)

    final = lax.fori_loop(0, size, eliminate, augmented)
    return jnp.transpose(final[:, size, :], (1, 0))


def general(observed, jacobian, tile_block, params, damping):
    ngx, ngy = lax.axis_size("gx"), lax.axis_size("gy")
    moved = flipped(observed, ("gx", "gy"), ngx * ngy)[::-1, ::-1]
    block_ids = jnp.arange(NB, dtype=jnp.int32)
    onehot = (tile_block[:, None] == block_ids[None, :]).astype(jnp.float32)
    tile_params = jnp.dot(onehot, params, precision=lax.Precision.HIGHEST).astype(jnp.bfloat16)
    calc = jnp.einsum("tpv,tp->tv", jacobian, tile_params, preferred_element_type=jnp.float32)
    resid = 0.5 * (observed + moved) - calc
    local_misfit = jnp.sum(resid * resid)
    resid_b = resid.astype(jnp.bfloat16)
    tile_grad = jnp.einsum("tpv,tv->tp", jacobian, resid_b, preferred_element_type=jnp.float32)
    tile_gram = jnp.einsum("tpv,tqv->tpq", jacobian, jacobian, preferred_element_type=jnp.float32)
    gram = jnp.einsum("tb,tpq->bpq", onehot, tile_gram, precision=lax.Precision.HIGHEST)
    grad = jnp.dot(onehot.T, tile_grad, precision=lax.Precision.HIGHEST)
    owned = NB // ngy
    gram, grad, total = lax.psum((gram, grad, local_misfit), ("gx", "gy"))
    first = lax.axis_index("gy") * owned
    gram = lax.dynamic_slice_in_dim(gram, first, owned, 0)
    grad = lax.dynamic_slice_in_dim(grad, first, owned, 0)
    diagonal = jnp.diagonal(gram, axis1=1, axis2=2)
    eye = jnp.eye(gram.shape[1], dtype=jnp.float32)
    system = gram + damping[0] * diagonal[:, :, None] * eye[None] + eye[None]
    delta = solve_blocks(system, grad)
    return delta * jnp.sqrt(diagonal), total / (observed.size * ngx * ngy)


def solution(mesh):
    ngx, ngy = mesh.shape["gx"], mesh.shape["gy"]
    quick = ngy == 2 and ngx > PLANE and ngx & (ngx - 1) == 0 and NB % (2 * ngx * ngy) == 0
    return jax.shard_map(
        fast if quick else general,
        mesh=mesh,
        in_specs=(P(("gx", "gy"), None), P(("gx", "gy"), None, None), P(("gx", "gy")), P(), P()),
        out_specs=(P("gy", None), P()),
        check_vma=False,
    )
```

time: 75.6 us -> 64.2 us (0.85)
  Pallas kernels: 22.3 us -> 13.9 us
  local copies, waits for them, and re-layouts: 3.71 us -> 1.18 us
  other arithmetic: 2.04 us -> 0.13 us
  waiting for transfers between devices: 18.6 us -> 20.2 us
    pallas_call x2, Pallas kernels: 18.1 us -> 10.4 us  [the longest x1 7.15 us: fast_inner(): pl.pallas_call(gram_body, out_shape=(pltpu.VMEM((2, side_tiles, vox), jnp...]
    unnamed x7 -> x5, local copies, waits for them, and re-layouts: 1.89 us -> 0.62 us
    add x1, other arithmetic: 1.12 us -> 0.06 us  [fast_inner(): mine = keep + xored(send, 'gy', 1)]
    ppermute x1, waiting for transfers between devices: 2.77 us -> 3.82 us  [flipped(): return lax.ppermute(value, axes, [(i, size - 1 - i) for i in range(size)])]
    add x1, other arithmetic: 0.85 us -> 0.01 us  [fast_inner(): rest = plane(keep + xored(send, 'gy', 1))]
  transfers between devices with their start and end apart: 12 -> 12, of which waited for: 8 -> 8; matrix products, arithmetic and copies ran while one was open for 3% -> 1% of each run, Pallas kernels for 0% -> 0%
where the time goes in v1:
time: 64.2 us; the launch traced here: 64 us
  starting transfers between devices  25.5 us (40%)
  waiting for transfers between devices  20.2 us (31%)
  Pallas kernels  13.9 us (22%)
  between operations  3.16 us (5%)
  local copies, waits for them, and re-layouts  1.18 us (2%)
    ppermute x10, starting transfers between devices, xored(): lax.ppermute(value, axis, [(i, i ^ bit) for i in range(lax.axis_size(axis...  13.9 us
    ppermute x10, waiting for transfers between devices, xored(): lax.ppermute(value, axis, [(i, i ^ bit) for i in range(lax.axis_size(axis...  10.1 us
    pallas_call x1, Pallas kernels, fast_inner(): pl.pallas_call(gram_body, out_shape=(pltpu.VMEM((2, side_tiles, vox), jnp...  7.15 us
    ppermute x1, starting transfers between devices, flipped(): return lax.ppermute(value, axes, [(i, size - 1 - i) for i in range(size)])  6.58 us
    all_to_all x1, waiting for transfers between devices, fast_inner(): every = lax.all_to_all(step, 'gx', 0, 0)  6.24 us
    all_to_all x1, starting transfers between devices, fast_inner(): every = lax.all_to_all(step, 'gx', 0, 0)  5.06 us
    ppermute x1, waiting for transfers between devices, flipped(): return lax.ppermute(value, axes, [(i, size - 1 - i) for i in range(size)])  3.82 us
    pallas_call x1, Pallas kernels, fast_inner(): pl.pallas_call(solve_body, out_shape=(jax.ShapeDtypeStruct((ngx, per, vox...  3.5 us
  transfers between devices with their start and end apart: 12, of which 8 were waited for; matrix products, arithmetic and copies ran while one was open for 1% of the time, Pallas kernels for 0%

profile of v1, /device:TPU:0, one launch (start us, length us, event | category | flops | bytes accessed | tf_op | source)
XLA Modules:
  0.0 64.0 jit_solution(10680485981515522323)
XLA Ops:
  0.6 0.0 copy-start.1
  0.6 0.0 copy-start
  0.7 7.2 %gram.1 = (f32[2,128,128]{2,1,0:T(8,128)S(1)}, f32[16,64,128]{2,1,0:T(8,128)S(1)}, f32[16,64,128]{2,1,0:T(8,128)S(1)}, f32[2,16,2,128]{3,2,1,0:T(2,128)S(1)}, bf16[2,128,64,128]{3,2,1,0:T(8,128)(2,1)S(1)}) custom-call(s32[256]{0:T(256)} %tb.1, bf16[2,128,64,128]{3,2,1,0:T(8,128)(2,1)} %bitcast.11, f32[64,128]{1,0:T(8,128)} %bitcast.13), custom_call_target="tpu_custom_call" | custom-call | tf_op jit(solution)/shard_map/gram/pallas_call | solution.py:300
  7.8 0.6 collective-permute-start
  8.4 0.0 copy-done
  8.4 6.6 %collective-permute-start.4 = (f32[256,128]{1,0:T(8,128)S(1)}, f32[256,128]{1,0:T(8,128)S(1)}, u32[]{:S(2)}, u32[]{:S(2)}) collective-permute-start(f32[256,128]{1,0:T(8,128)S(1)} %copy-done), channel_id=1, source_target_pairs={{0,31},{1,30},{2,29},{3,28},{4,27},{5,26},{6,25},{7,24},{8,23},{9,... | collective-permute-start | bytes 393224 | tf_op jit(solution)/shard_map/ppermute | solution.py:21
  14.9 0.0 collective-permute-done
  14.9 0.1 add.27
  15.0 3.8 %collective-permute-done.4 = f32[256,128]{1,0:T(8,128)S(1)} collective-permute-done((f32[256,128]{1,0:T(8,128)S(1)}, f32[256,128]{1,0:T(8,128)S(1)}, u32[]{:S(2)}, u32[]{:S(2)}) %collective-permute-start.4) | collective-permute-done | bytes 131104 | tf_op jit(solution)/shard_map/ppermute | solution.py:21
  18.8 0.0 copy-done.1
  18.8 3.2 %grad.1 = (f32[16,8,128]{2,1,0:T(8,128)S(1)}, f32[16,8,128]{2,1,0:T(8,128)S(1)}) custom-call(s32[2,128]{1,0:T(2,128)S(1)} %bitcast.10, bf16[2,128,64,128]{3,2,1,0:T(8,128)(2,1)S(1)} %get-tuple-element.17.jbuf, f32[2,128,128]{2,1,0:T(8,128)S(1)} %get-tuple-element.18.calc_ref, f32[2,128,128]{2,1,0:T(8,128)S(1)} %bitcast.8, f32[2,128,128]{2,1,0:T(8,128)S(1)} %bitcast.9, ...), custom_call_target="tpu_custom_call" | custom-call | tf_op jit(solution)/shard_map/grad/pallas_call | solution.py:322
  22.1 0.2 collective-permute-start.5
  22.2 1.2 %collective-permute-done.5 = f32[16,8,128]{2,1,0:T(8,128)S(1)} collective-permute-done((f32[16,8,128]{2,1,0:T(8,128)S(1)}, f32[16,8,128]{2,1,0:T(8,128)S(1)}, u32[]{:S(2)}, u32[]{:S(2)}) %collective-permute-start.5) | collective-permute-done | bytes 65568 | tf_op jit(solution)/shard_map/ppermute | solution.py:25
  23.4 1.1 %collective-permute-start.6 = (f32[4,8,128]{2,1,0:T(8,128)S(1)}, f32[4,8,128]{2,1,0:T(8,128)S(1)}, u32[]{:S(2)}, u32[]{:S(2)}) collective-permute-start(f32[4,8,128]{2,1,0:T(8,128)S(1)} %get-tuple-element.29), channel_id=1, source_target_pairs={{0,2},{2,0},{4,6},{6,4},{8,10},{10,8},{12,14},{14,12},{16,18},{18,... | collective-permute-start | bytes 49160 | tf_op jit(solution)/shard_map/ppermute | solution.py:25
  24.5 1.5 %collective-permute-start.7 = (f32[4,8,128]{2,1,0:T(8,128)S(1)}, f32[4,8,128]{2,1,0:T(8,128)S(1)}, u32[]{:S(2)}, u32[]{:S(2)}) collective-permute-start(f32[4,8,128]{2,1,0:T(8,128)S(1)} %get-tuple-element.31), channel_id=1, source_target_pairs={{0,4},{2,6},{4,0},{6,2},{8,12},{10,14},{12,8},{14,10},{16,20},{18,... | collective-permute-start | bytes 49160 | tf_op jit(solution)/shard_map/ppermute | solution.py:25
  26.1 0.9 %collective-permute-start.8 = (f32[4,8,128]{2,1,0:T(8,128)S(1)}, f32[4,8,128]{2,1,0:T(8,128)S(1)}, u32[]{:S(2)}, u32[]{:S(2)}) collective-permute-start(f32[4,8,128]{2,1,0:T(8,128)S(1)} %get-tuple-element.30), channel_id=1, source_target_pairs={{0,6},{2,4},{4,2},{6,0},{8,14},{10,12},{12,10},{14,8},{16,22},{18,... | collective-permute-start | bytes 49160 | tf_op jit(solution)/shard_map/ppermute | solution.py:25
  27.0 1.1 %collective-permute-start.1 = (f32[4,64,128]{2,1,0:T(8,128)S(1)}, f32[4,64,128]{2,1,0:T(8,128)S(1)}, u32[]{:S(2)}, u32[]{:S(2)}) collective-permute-start(f32[4,64,128]{2,1,0:T(8,128)S(1)} %get-tuple-element.24), channel_id=1, source_target_pairs={{0,2},{2,0},{4,6},{6,4},{8,10},{10,8},{12,14},{14,12},{16,18},{18,... | collective-permute-start | bytes 393224 | tf_op jit(solution)/shard_map/ppermute | solution.py:25
  28.1 1.5 %collective-permute-start.2 = (f32[4,64,128]{2,1,0:T(8,128)S(1)}, f32[4,64,128]{2,1,0:T(8,128)S(1)}, u32[]{:S(2)}, u32[]{:S(2)}) collective-permute-start(f32[4,64,128]{2,1,0:T(8,128)S(1)} %get-tuple-element.26), channel_id=1, source_target_pairs={{0,4},{2,6},{4,0},{6,2},{8,12},{10,14},{12,8},{14,10},{16,20},{18,... | collective-permute-start | bytes 393224 | tf_op jit(solution)/shard_map/ppermute | solution.py:25
  29.6 0.0 collective-permute-done.6
  29.6 0.9 %collective-permute-start.3 = (f32[4,64,128]{2,1,0:T(8,128)S(1)}, f32[4,64,128]{2,1,0:T(8,128)S(1)}, u32[]{:S(2)}, u32[]{:S(2)}) collective-permute-start(f32[4,64,128]{2,1,0:T(8,128)S(1)} %get-tuple-element.25), channel_id=1, source_target_pairs={{0,6},{2,4},{4,2},{6,0},{8,14},{10,12},{12,10},{14,8},{16,22},{18,... | collective-permute-start | bytes 393224 | tf_op jit(solution)/shard_map/ppermute | solution.py:25
  30.6 0.0 collective-permute-done.7
  30.6 0.3 collective-permute-done.8
  30.9 2.1 %collective-permute-done.1 = f32[4,64,128]{2,1,0:T(8,128)S(1)} collective-permute-done((f32[4,64,128]{2,1,0:T(8,128)S(1)}, f32[4,64,128]{2,1,0:T(8,128)S(1)}, u32[]{:S(2)}, u32[]{:S(2)}) %collective-permute-start.1) | collective-permute-done | bytes 131104 | tf_op jit(solution)/shard_map/ppermute | solution.py:25
  32.9 3.0 %collective-permute-done.2 = f32[4,64,128]{2,1,0:T(8,128)S(1)} collective-permute-done((f32[4,64,128]{2,1,0:T(8,128)S(1)}, f32[4,64,128]{2,1,0:T(8,128)S(1)}, u32[]{:S(2)}, u32[]{:S(2)}) %collective-permute-start.2) | collective-permute-done | bytes 131104 | tf_op jit(solution)/shard_map/ppermute | solution.py:25
  35.9 0.0 collective-permute-done.3
  35.9 2.6 %collective-permute-start.9 = (f32[2,72,128]{2,1,0:T(8,128)S(1)}, f32[2,72,128]{2,1,0:T(8,128)S(1)}, u32[]{:S(2)}, u32[]{:S(2)}) collective-permute-start(f32[2,72,128]{2,1,0:T(8,128)S(1)} %pad_maximum_fusion), channel_id=1, source_target_pairs={{0,8},{2,10},{4,12},{6,14},{8,0},{10,2},{12,4},{14,6},{16,24},{18,... | collective-permute-start | bytes 221192 | tf_op jit(solution)/shard_map/ppermute | solution.py:25
  38.5 2.3 %collective-permute-done.9 = f32[2,72,128]{2,1,0:T(8,128)S(1)} collective-permute-done((f32[2,72,128]{2,1,0:T(8,128)S(1)}, f32[2,72,128]{2,1,0:T(8,128)S(1)}, u32[]{:S(2)}, u32[]{:S(2)}) %collective-permute-start.9) | collective-permute-done | bytes 73760 | tf_op jit(solution)/shard_map/ppermute | solution.py:25
  40.9 3.5 %collective-permute-start.10 = (f32[1,72,128]{2,1,0:T(8,128)S(1)}, f32[1,72,128]{2,1,0:T(8,128)S(1)}, u32[]{:S(2)}, u32[]{:S(2)}) collective-permute-start(f32[1,72,128]{2,1,0:T(8,128)S(1)} %get-tuple-element.27), channel_id=1, source_target_pairs={{0,16},{2,18},{4,20},{6,22},{8,24},{10,26},{12,28},{14,30},{16,0},... | collective-permute-start | bytes 110600 | tf_op jit(solution)/shard_map/ppermute | solution.py:25
  45.0 1.3 %collective-permute-done.10.b_ref = f32[1,72,128]{2,1,0:T(8,128)S(1)} collective-permute-done((f32[1,72,128]{2,1,0:T(8,128)S(1)}, f32[1,72,128]{2,1,0:T(8,128)S(1)}, u32[]{:S(2)}, u32[]{:S(2)}) %collective-permute-start.10) | collective-permute-done | bytes 36896 | tf_op jit(solution)/shard_map/ppermute | solution.py:25
  46.3 3.5 %solve.1 = (f32[16,4,128]{2,1,0:T(4,128)}, f32[8,128]{1,0:T(8,128)S(1)}) custom-call(f32[1]{0:T(128)S(6)} %copy.8.damp, f32[1,72,128]{2,1,0:T(8,128)S(1)} %get-tuple-element.28.a_ref, f32[1,72,128]{2,1,0:T(8,128)S(1)} %collective-permute-done.10.b_ref), custom_call_target="tpu_custom_call" | custom-call | tf_op jit(solution)/shard_map/solve/pallas_call | solution.py:338
  49.8 5.1 %all-to-all-start = ((f32[16,4,128]{2,1,0:T(4,128)}), f32[16,4,128]{2,1,0:T(4,128)S(1)}, u32[]{:S(2)}, u32[]{:S(2)}) async-start(f32[16,4,128]{2,1,0:T(4,128)} %get-tuple-element.22), calls=%async_computation | async-start | bytes 65536 | tf_op jit(solution)/shard_map/all_to_all | solution.py:346
  54.9 0.5 slice.63
  56.0 6.2 %all-to-all-done = f32[16,4,128]{2,1,0:T(4,128)S(1)} async-done(((f32[16,4,128]{2,1,0:T(4,128)}), f32[16,4,128]{2,1,0:T(4,128)S(1)}, u32[]{:S(2)}, u32[]{:S(2)}) %all-to-all-start) | async-done | bytes 32800 | tf_op jit(solution)/shard_map/all_to_all | solution.py:346
  62.3 0.6 copy.9
  (8 shorter events, 0.1 us)
Async XLA Ops:
  0.6 18.2 %copy-start.1 = (s32[256]{0:T(256)S(1)}, s32[256]{0:T(256)}, u32[]{:S(2)}) copy-start(s32[256]{0:T(256)} %tb.1) | copy-start | bytes 3076
  0.6 7.7 %copy-start = (f32[256,128]{1,0:T(8,128)S(1)}, f32[256,128]{1,0:T(8,128)}, u32[]{:S(2)}) copy-start(f32[256,128]{1,0:T(8,128)} %param.5) | copy-start | bytes 393220
  7.8 7.1 %collective-permute-start = (f32[16,64,128]{2,1,0:T(8,128)S(1)}, f32[16,64,128]{2,1,0:T(8,128)S(1)}, u32[]{:S(2)}, u32[]{:S(2)}) collective-permute-start(f32[16,64,128]{2,1,0:T(8,128)S(1)} %get-tuple-element.15), channel_id=1, source_target_pairs={{0,1},{1,0},{2,3},{3,2},{4,5},{5,4},{6,7},{7,6},{8,9},{9,8},{10,11... | collective-permute-start | bytes 1572872 | tf_op jit(solution)/shard_map/ppermute | solution.py:25
  8.4 10.5 %collective-permute-start.4 = (f32[256,128]{1,0:T(8,128)S(1)}, f32[256,128]{1,0:T(8,128)S(1)}, u32[]{:S(2)}, u32[]{:S(2)}) collective-permute-start(f32[256,128]{1,0:T(8,128)S(1)} %copy-done), channel_id=1, source_target_pairs={{0,31},{1,30},{2,29},{3,28},{4,27},{5,26},{6,25},{7,24},{8,23},{9,... | collective-permute-start | bytes 393224 | tf_op jit(solution)/shard_map/ppermute | solution.py:21
  22.1 1.3 %collective-permute-start.5 = (f32[16,8,128]{2,1,0:T(8,128)S(1)}, f32[16,8,128]{2,1,0:T(8,128)S(1)}, u32[]{:S(2)}, u32[]{:S(2)}) collective-permute-start(f32[16,8,128]{2,1,0:T(8,128)S(1)} %get-tuple-element.21), channel_id=1, source_target_pairs={{0,1},{1,0},{2,3},{3,2},{4,5},{5,4},{6,7},{7,6},{8,9},{9,8},{10,11... | collective-permute-start | bytes 196616 | tf_op jit(solution)/shard_map/ppermute | solution.py:25
  23.4 6.2 %collective-permute-start.6 = (f32[4,8,128]{2,1,0:T(8,128)S(1)}, f32[4,8,128]{2,1,0:T(8,128)S(1)}, u32[]{:S(2)}, u32[]{:S(2)}) collective-permute-start(f32[4,8,128]{2,1,0:T(8,128)S(1)} %get-tuple-element.29), channel_id=1, source_target_pairs={{0,2},{2,0},{4,6},{6,4},{8,10},{10,8},{12,14},{14,12},{16,18},{18,... | collective-permute-start | bytes 49160 | tf_op jit(solution)/shard_map/ppermute | solution.py:25
  24.5 6.0 %collective-permute-start.7 = (f32[4,8,128]{2,1,0:T(8,128)S(1)}, f32[4,8,128]{2,1,0:T(8,128)S(1)}, u32[]{:S(2)}, u32[]{:S(2)}) collective-permute-start(f32[4,8,128]{2,1,0:T(8,128)S(1)} %get-tuple-element.31), channel_id=1, source_target_pairs={{0,4},{2,6},{4,0},{6,2},{8,12},{10,14},{12,8},{14,10},{16,20},{18,... | collective-permute-start | bytes 49160 | tf_op jit(solution)/shard_map/ppermute | solution.py:25
  26.1 4.8 %collective-permute-start.8 = (f32[4,8,128]{2,1,0:T(8,128)S(1)}, f32[4,8,128]{2,1,0:T(8,128)S(1)}, u32[]{:S(2)}, u32[]{:S(2)}) collective-permute-start(f32[4,8,128]{2,1,0:T(8,128)S(1)} %get-tuple-element.30), channel_id=1, source_target_pairs={{0,6},{2,4},{4,2},{6,0},{8,14},{10,12},{12,10},{14,8},{16,22},{18,... | collective-permute-start | bytes 49160 | tf_op jit(solution)/shard_map/ppermute | solution.py:25
  27.0 5.9 %collective-permute-start.1 = (f32[4,64,128]{2,1,0:T(8,128)S(1)}, f32[4,64,128]{2,1,0:T(8,128)S(1)}, u32[]{:S(2)}, u32[]{:S(2)}) collective-permute-start(f32[4,64,128]{2,1,0:T(8,128)S(1)} %get-tuple-element.24), channel_id=1, source_target_pairs={{0,2},{2,0},{4,6},{6,4},{8,10},{10,8},{12,14},{14,12},{16,18},{18,... | collective-permute-start | bytes 393224 | tf_op jit(solution)/shard_map/ppermute | solution.py:25
  28.1 7.8 %collective-permute-start.2 = (f32[4,64,128]{2,1,0:T(8,128)S(1)}, f32[4,64,128]{2,1,0:T(8,128)S(1)}, u32[]{:S(2)}, u32[]{:S(2)}) collective-permute-start(f32[4,64,128]{2,1,0:T(8,128)S(1)} %get-tuple-element.26), channel_id=1, source_target_pairs={{0,4},{2,6},{4,0},{6,2},{8,12},{10,14},{12,8},{14,10},{16,20},{18,... | collective-permute-start | bytes 393224 | tf_op jit(solution)/shard_map/ppermute | solution.py:25
  29.6 6.2 %collective-permute-start.3 = (f32[4,64,128]{2,1,0:T(8,128)S(1)}, f32[4,64,128]{2,1,0:T(8,128)S(1)}, u32[]{:S(2)}, u32[]{:S(2)}) collective-permute-start(f32[4,64,128]{2,1,0:T(8,128)S(1)} %get-tuple-element.25), channel_id=1, source_target_pairs={{0,6},{2,4},{4,2},{6,0},{8,14},{10,12},{12,10},{14,8},{16,22},{18,... | collective-permute-start | bytes 393224 | tf_op jit(solution)/shard_map/ppermute | solution.py:25
  35.9 4.9 %collective-permute-start.9 = (f32[2,72,128]{2,1,0:T(8,128)S(1)}, f32[2,72,128]{2,1,0:T(8,128)S(1)}, u32[]{:S(2)}, u32[]{:S(2)}) collective-permute-start(f32[2,72,128]{2,1,0:T(8,128)S(1)} %pad_maximum_fusion), channel_id=1, source_target_pairs={{0,8},{2,10},{4,12},{6,14},{8,0},{10,2},{12,4},{14,6},{16,24},{18,... | collective-permute-start | bytes 221192 | tf_op jit(solution)/shard_map/ppermute | solution.py:25
  40.9 5.4 %collective-permute-start.10 = (f32[1,72,128]{2,1,0:T(8,128)S(1)}, f32[1,72,128]{2,1,0:T(8,128)S(1)}, u32[]{:S(2)}, u32[]{:S(2)}) collective-permute-start(f32[1,72,128]{2,1,0:T(8,128)S(1)} %get-tuple-element.27), channel_id=1, source_target_pairs={{0,16},{2,18},{4,20},{6,22},{8,24},{10,26},{12,28},{14,30},{16,0},... | collective-permute-start | bytes 110600 | tf_op jit(solution)/shard_map/ppermute | solution.py:25
  49.8 12.5 %all-to-all-start = ((f32[16,4,128]{2,1,0:T(4,128)}), f32[16,4,128]{2,1,0:T(4,128)S(1)}, u32[]{:S(2)}, u32[]{:S(2)}) async-start(f32[16,4,128]{2,1,0:T(4,128)} %get-tuple-element.22), calls=%async_computation | async-start | bytes 65536 | tf_op jit(solution)/shard_map/all_to_all | solution.py:346

commit v2 on v1

--- a/solution.py
+++ b/solution.py
@@ -316,9 +316,8 @@
         compiler_params=limit,
         name="gram",
     )(far(tile_block), far(halved(jacobian)), far(params.T))
-    mine = keep + xored(send, "gy", 1)
-    tied, mine = lax.optimization_barrier((calc, mine))
-    got = plane(mine)
+    other = xored(send, "gy", 1)
+    got = plane(keep + other)
     keep, send = pl.pallas_call(
         grad_body,
         out_shape=(extra, extra),
@@ -327,8 +326,10 @@
         scratch_shapes=[pltpu.VMEM((side_tiles, vox), jnp.float32), pltpu.VMEM((NB, vox), jnp.float32)],
         compiler_params=limit,
         name="grad",
-    )(halved(tile_block), local(staged), local(tied), halved(observed), local(halved(moved)), local(diag))
-    rest = plane(keep + xored(send, "gy", 1))
+    )(halved(tile_block), local(staged), local(calc), halved(observed), local(halved(moved)), local(diag))
+    other = xored(send, "gy", 1)
+    both = keep + other
+    rest = plane(both)
     both = jnp.concatenate([got, rest], axis=1)
     mine, got = both, jnp.zeros_like(both)
     for s in range(PLANE.bit_length() - 1, bits):

time: 64.2 us -> 64.3 us (level)
  transfers between devices with their start and end apart: 12 -> 12, of which waited for: 8 -> 8; matrix products, arithmetic and copies ran while one was open for 1% -> 1% of each run, Pallas kernels for 0% -> 5%
where the time goes in v2:
time: 64.3 us; the launch traced here: 64.1 us
  starting transfers between devices  25.5 us (40%)
  waiting for transfers between devices  20.2 us (31%)
  Pallas kernels  13.9 us (22%)
  between operations  3.16 us (5%)
  local copies, waits for them, and re-layouts  1.18 us (2%)
    ppermute x10, starting transfers between devices, xored(): lax.ppermute(value, axis, [(i, i ^ bit) for i in range(lax.axis_size(axis...  13.9 us
    ppermute x10, waiting for transfers between devices, xored(): lax.ppermute(value, axis, [(i, i ^ bit) for i in range(lax.axis_size(axis...  10.1 us
    pallas_call x1, Pallas kernels, fast_inner(): pl.pallas_call(gram_body, out_shape=(pltpu.VMEM((2, side_tiles, vox), jnp...  7.15 us
    ppermute x1, starting transfers between devices, flipped(): return lax.ppermute(value, axes, [(i, size - 1 - i) for i in range(size)])  6.58 us
    all_to_all x1, waiting for transfers between devices, fast_inner(): every = lax.all_to_all(step, 'gx', 0, 0)  6.24 us
    all_to_all x1, starting transfers between devices, fast_inner(): every = lax.all_to_all(step, 'gx', 0, 0)  5.06 us
    ppermute x1, waiting for transfers between devices, flipped(): return lax.ppermute(value, axes, [(i, size - 1 - i) for i in range(size)])  3.89 us
    pallas_call x1, Pallas kernels, fast_inner(): pl.pallas_call(solve_body, out_shape=(jax.ShapeDtypeStruct((ngx, per, vox...  3.5 us
  transfers between devices with their start and end apart: 12, of which 8 were waited for; matrix products, arithmetic and copies ran while one was open for 1% of the time, Pallas kernels for 5%

profile of v2, /device:TPU:0, one launch (start us, length us, event | category | flops | bytes accessed | tf_op | source)
XLA Modules:
  0.0 64.1 jit_solution(16824035219608012637)
XLA Ops:
  0.6 0.0 copy-start.1
  0.6 0.0 copy-start
  0.7 7.2 %gram.1 = (f32[2,128,128]{2,1,0:T(8,128)S(1)}, f32[16,64,128]{2,1,0:T(8,128)S(1)}, f32[16,64,128]{2,1,0:T(8,128)S(1)}, f32[2,16,2,128]{3,2,1,0:T(2,128)S(1)}, bf16[2,128,64,128]{3,2,1,0:T(8,128)(2,1)S(1)}) custom-call(s32[256]{0:T(256)} %tb.1, bf16[2,128,64,128]{3,2,1,0:T(8,128)(2,1)} %bitcast.11, f32[64,128]{1,0:T(8,128)} %bitcast.13), custom_call_target="tpu_custom_call" | custom-call | tf_op jit(solution)/shard_map/gram/pallas_call | solution.py:300
  7.8 0.6 collective-permute-start
  8.4 0.0 copy-done
  8.4 6.6 %collective-permute-start.4 = (f32[256,128]{1,0:T(8,128)S(1)}, f32[256,128]{1,0:T(8,128)S(1)}, u32[]{:S(2)}, u32[]{:S(2)}) collective-permute-start(f32[256,128]{1,0:T(8,128)S(1)} %copy-done), channel_id=1, source_target_pairs={{0,31},{1,30},{2,29},{3,28},{4,27},{5,26},{6,25},{7,24},{8,23},{9,... | collective-permute-start | bytes 393224 | tf_op jit(solution)/shard_map/ppermute | solution.py:21
  14.9 3.9 %collective-permute-done.4 = f32[256,128]{1,0:T(8,128)S(1)} collective-permute-done((f32[256,128]{1,0:T(8,128)S(1)}, f32[256,128]{1,0:T(8,128)S(1)}, u32[]{:S(2)}, u32[]{:S(2)}) %collective-permute-start.4) | collective-permute-done | bytes 131104 | tf_op jit(solution)/shard_map/ppermute | solution.py:21
  18.8 0.0 copy-done.1
  18.8 3.2 %grad.1 = (f32[16,8,128]{2,1,0:T(8,128)S(1)}, f32[16,8,128]{2,1,0:T(8,128)S(1)}) custom-call(s32[2,128]{1,0:T(2,128)S(1)} %bitcast.10, bf16[2,128,64,128]{3,2,1,0:T(8,128)(2,1)S(1)} %get-tuple-element.13.jbuf, f32[2,128,128]{2,1,0:T(8,128)S(1)} %get-tuple-element.14.calc_ref, f32[2,128,128]{2,1,0:T(8,128)S(1)} %bitcast.8, f32[2,128,128]{2,1,0:T(8,128)S(1)} %bitcast.9, ...), custom_call_target="tpu_custom_call" | custom-call | tf_op jit(solution)/shard_map/grad/pallas_call | solution.py:321
  22.1 0.2 collective-permute-start.5
  22.2 1.2 %collective-permute-done.5 = f32[16,8,128]{2,1,0:T(8,128)S(1)} collective-permute-done((f32[16,8,128]{2,1,0:T(8,128)S(1)}, f32[16,8,128]{2,1,0:T(8,128)S(1)}, u32[]{:S(2)}, u32[]{:S(2)}) %collective-permute-start.5) | collective-permute-done | bytes 65568 | tf_op jit(solution)/shard_map/ppermute | solution.py:25
  23.4 1.1 %collective-permute-start.6 = (f32[4,8,128]{2,1,0:T(8,128)S(1)}, f32[4,8,128]{2,1,0:T(8,128)S(1)}, u32[]{:S(2)}, u32[]{:S(2)}) collective-permute-start(f32[4,8,128]{2,1,0:T(8,128)S(1)} %get-tuple-element.25), channel_id=1, source_target_pairs={{0,2},{2,0},{4,6},{6,4},{8,10},{10,8},{12,14},{14,12},{16,18},{18,... | collective-permute-start | bytes 49160 | tf_op jit(solution)/shard_map/ppermute | solution.py:25
  24.5 1.5 %collective-permute-start.7 = (f32[4,8,128]{2,1,0:T(8,128)S(1)}, f32[4,8,128]{2,1,0:T(8,128)S(1)}, u32[]{:S(2)}, u32[]{:S(2)}) collective-permute-start(f32[4,8,128]{2,1,0:T(8,128)S(1)} %get-tuple-element.27), channel_id=1, source_target_pairs={{0,4},{2,6},{4,0},{6,2},{8,12},{10,14},{12,8},{14,10},{16,20},{18,... | collective-permute-start | bytes 49160 | tf_op jit(solution)/shard_map/ppermute | solution.py:25
  26.1 0.9 %collective-permute-start.8 = (f32[4,8,128]{2,1,0:T(8,128)S(1)}, f32[4,8,128]{2,1,0:T(8,128)S(1)}, u32[]{:S(2)}, u32[]{:S(2)}) collective-permute-start(f32[4,8,128]{2,1,0:T(8,128)S(1)} %get-tuple-element.26), channel_id=1, source_target_pairs={{0,6},{2,4},{4,2},{6,0},{8,14},{10,12},{12,10},{14,8},{16,22},{18,... | collective-permute-start | bytes 49160 | tf_op jit(solution)/shard_map/ppermute | solution.py:25
  27.0 0.0 collective-permute-done
  27.0 0.1 add.27
  27.1 1.1 %collective-permute-start.1 = (f32[4,64,128]{2,1,0:T(8,128)S(1)}, f32[4,64,128]{2,1,0:T(8,128)S(1)}, u32[]{:S(2)}, u32[]{:S(2)}) collective-permute-start(f32[4,64,128]{2,1,0:T(8,128)S(1)} %get-tuple-element.20), channel_id=1, source_target_pairs={{0,2},{2,0},{4,6},{6,4},{8,10},{10,8},{12,14},{14,12},{16,18},{18,... | collective-permute-start | bytes 393224 | tf_op jit(solution)/shard_map/ppermute | solution.py:25
  28.2 1.5 %collective-permute-start.2 = (f32[4,64,128]{2,1,0:T(8,128)S(1)}, f32[4,64,128]{2,1,0:T(8,128)S(1)}, u32[]{:S(2)}, u32[]{:S(2)}) collective-permute-start(f32[4,64,128]{2,1,0:T(8,128)S(1)} %get-tuple-element.22), channel_id=1, source_target_pairs={{0,4},{2,6},{4,0},{6,2},{8,12},{10,14},{12,8},{14,10},{16,20},{18,... | collective-permute-start | bytes 393224 | tf_op jit(solution)/shard_map/ppermute | solution.py:25
  29.7 0.0 collective-permute-done.6
  29.7 0.9 %collective-permute-start.3 = (f32[4,64,128]{2,1,0:T(8,128)S(1)}, f32[4,64,128]{2,1,0:T(8,128)S(1)}, u32[]{:S(2)}, u32[]{:S(2)}) collective-permute-start(f32[4,64,128]{2,1,0:T(8,128)S(1)} %get-tuple-element.21), channel_id=1, source_target_pairs={{0,6},{2,4},{4,2},{6,0},{8,14},{10,12},{12,10},{14,8},{16,22},{18,... | collective-permute-start | bytes 393224 | tf_op jit(solution)/shard_map/ppermute | solution.py:25
  30.6 0.0 collective-permute-done.7
  30.6 0.2 collective-permute-done.8
  30.9 2.1 %collective-permute-done.1 = f32[4,64,128]{2,1,0:T(8,128)S(1)} collective-permute-done((f32[4,64,128]{2,1,0:T(8,128)S(1)}, f32[4,64,128]{2,1,0:T(8,128)S(1)}, u32[]{:S(2)}, u32[]{:S(2)}) %collective-permute-start.1) | collective-permute-done | bytes 131104 | tf_op jit(solution)/shard_map/ppermute | solution.py:25
  33.0 3.0 %collective-permute-done.2 = f32[4,64,128]{2,1,0:T(8,128)S(1)} collective-permute-done((f32[4,64,128]{2,1,0:T(8,128)S(1)}, f32[4,64,128]{2,1,0:T(8,128)S(1)}, u32[]{:S(2)}, u32[]{:S(2)}) %collective-permute-start.2) | collective-permute-done | bytes 131104 | tf_op jit(solution)/shard_map/ppermute | solution.py:25
  36.0 0.0 collective-permute-done.3
  36.0 2.6 %collective-permute-start.9 = (f32[2,72,128]{2,1,0:T(8,128)S(1)}, f32[2,72,128]{2,1,0:T(8,128)S(1)}, u32[]{:S(2)}, u32[]{:S(2)}) collective-permute-start(f32[2,72,128]{2,1,0:T(8,128)S(1)} %pad_maximum_fusion), channel_id=1, source_target_pairs={{0,8},{2,10},{4,12},{6,14},{8,0},{10,2},{12,4},{14,6},{16,24},{18,... | collective-permute-start | bytes 221192 | tf_op jit(solution)/shard_map/ppermute | solution.py:25
  38.6 2.3 %collective-permute-done.9 = f32[2,72,128]{2,1,0:T(8,128)S(1)} collective-permute-done((f32[2,72,128]{2,1,0:T(8,128)S(1)}, f32[2,72,128]{2,1,0:T(8,128)S(1)}, u32[]{:S(2)}, u32[]{:S(2)}) %collective-permute-start.9) | collective-permute-done | bytes 73760 | tf_op jit(solution)/shard_map/ppermute | solution.py:25
  40.9 3.5 %collective-permute-start.10 = (f32[1,72,128]{2,1,0:T(8,128)S(1)}, f32[1,72,128]{2,1,0:T(8,128)S(1)}, u32[]{:S(2)}, u32[]{:S(2)}) collective-permute-start(f32[1,72,128]{2,1,0:T(8,128)S(1)} %get-tuple-element.23), channel_id=1, source_target_pairs={{0,16},{2,18},{4,20},{6,22},{8,24},{10,26},{12,28},{14,30},{16,0},... | collective-permute-start | bytes 110600 | tf_op jit(solution)/shard_map/ppermute | solution.py:25
  45.1 1.3 %collective-permute-done.10.b_ref = f32[1,72,128]{2,1,0:T(8,128)S(1)} collective-permute-done((f32[1,72,128]{2,1,0:T(8,128)S(1)}, f32[1,72,128]{2,1,0:T(8,128)S(1)}, u32[]{:S(2)}, u32[]{:S(2)}) %collective-permute-start.10) | collective-permute-done | bytes 36896 | tf_op jit(solution)/shard_map/ppermute | solution.py:25
  46.4 3.5 %solve.1 = (f32[16,4,128]{2,1,0:T(4,128)}, f32[8,128]{1,0:T(8,128)S(1)}) custom-call(f32[1]{0:T(128)S(6)} %copy.8.damp, f32[1,72,128]{2,1,0:T(8,128)S(1)} %get-tuple-element.24.a_ref, f32[1,72,128]{2,1,0:T(8,128)S(1)} %collective-permute-done.10.b_ref), custom_call_target="tpu_custom_call" | custom-call | tf_op jit(solution)/shard_map/solve/pallas_call | solution.py:339
  49.9 5.1 %all-to-all-start = ((f32[16,4,128]{2,1,0:T(4,128)}), f32[16,4,128]{2,1,0:T(4,128)S(1)}, u32[]{:S(2)}, u32[]{:S(2)}) async-start(f32[16,4,128]{2,1,0:T(4,128)} %get-tuple-element.18), calls=%async_computation | async-start | bytes 65536 | tf_op jit(solution)/shard_map/all_to_all | solution.py:347
  54.9 0.5 slice.63
  56.1 6.2 %all-to-all-done = f32[16,4,128]{2,1,0:T(4,128)S(1)} async-done(((f32[16,4,128]{2,1,0:T(4,128)}), f32[16,4,128]{2,1,0:T(4,128)S(1)}, u32[]{:S(2)}, u32[]{:S(2)}) %all-to-all-start) | async-done | bytes 32800 | tf_op jit(solution)/shard_map/all_to_all | solution.py:347
  62.3 0.6 copy.9
  (8 shorter events, 0.1 us)
Async XLA Ops:
  0.6 18.2 %copy-start.1 = (s32[256]{0:T(256)S(1)}, s32[256]{0:T(256)}, u32[]{:S(2)}) copy-start(s32[256]{0:T(256)} %tb.1) | copy-start | bytes 3076
  0.6 7.7 %copy-start = (f32[256,128]{1,0:T(8,128)S(1)}, f32[256,128]{1,0:T(8,128)}, u32[]{:S(2)}) copy-start(f32[256,128]{1,0:T(8,128)} %param.5) | copy-start | bytes 393220
  7.8 19.2 %collective-permute-start = (f32[16,64,128]{2,1,0:T(8,128)S(1)}, f32[16,64,128]{2,1,0:T(8,128)S(1)}, u32[]{:S(2)}, u32[]{:S(2)}) collective-permute-start(f32[16,64,128]{2,1,0:T(8,128)S(1)} %get-tuple-element.12), channel_id=1, source_target_pairs={{0,1},{1,0},{2,3},{3,2},{4,5},{5,4},{6,7},{7,6},{8,9},{9,8},{10,11... | collective-permute-start | bytes 1572872 | tf_op jit(solution)/shard_map/ppermute | solution.py:25
  8.4 10.5 %collective-permute-start.4 = (f32[256,128]{1,0:T(8,128)S(1)}, f32[256,128]{1,0:T(8,128)S(1)}, u32[]{:S(2)}, u32[]{:S(2)}) collective-permute-start(f32[256,128]{1,0:T(8,128)S(1)} %copy-done), channel_id=1, source_target_pairs={{0,31},{1,30},{2,29},{3,28},{4,27},{5,26},{6,25},{7,24},{8,23},{9,... | collective-permute-start | bytes 393224 | tf_op jit(solution)/shard_map/ppermute | solution.py:21
  22.1 1.3 %collective-permute-start.5 = (f32[16,8,128]{2,1,0:T(8,128)S(1)}, f32[16,8,128]{2,1,0:T(8,128)S(1)}, u32[]{:S(2)}, u32[]{:S(2)}) collective-permute-start(f32[16,8,128]{2,1,0:T(8,128)S(1)} %get-tuple-element.17), channel_id=1, source_target_pairs={{0,1},{1,0},{2,3},{3,2},{4,5},{5,4},{6,7},{7,6},{8,9},{9,8},{10,11... | collective-permute-start | bytes 196616 | tf_op jit(solution)/shard_map/ppermute | solution.py:25
  23.4 6.3 %collective-permute-start.6 = (f32[4,8,128]{2,1,0:T(8,128)S(1)}, f32[4,8,128]{2,1,0:T(8,128)S(1)}, u32[]{:S(2)}, u32[]{:S(2)}) collective-permute-start(f32[4,8,128]{2,1,0:T(8,128)S(1)} %get-tuple-element.25), channel_id=1, source_target_pairs={{0,2},{2,0},{4,6},{6,4},{8,10},{10,8},{12,14},{14,12},{16,18},{18,... | collective-permute-start | bytes 49160 | tf_op jit(solution)/shard_map/ppermute | solution.py:25
  24.5 6.1 %collective-permute-start.7 = (f32[4,8,128]{2,1,0:T(8,128)S(1)}, f32[4,8,128]{2,1,0:T(8,128)S(1)}, u32[]{:S(2)}, u32[]{:S(2)}) collective-permute-start(f32[4,8,128]{2,1,0:T(8,128)S(1)} %get-tuple-element.27), channel_id=1, source_target_pairs={{0,4},{2,6},{4,0},{6,2},{8,12},{10,14},{12,8},{14,10},{16,20},{18,... | collective-permute-start | bytes 49160 | tf_op jit(solution)/shard_map/ppermute | solution.py:25
  26.1 4.8 %collective-permute-start.8 = (f32[4,8,128]{2,1,0:T(8,128)S(1)}, f32[4,8,128]{2,1,0:T(8,128)S(1)}, u32[]{:S(2)}, u32[]{:S(2)}) collective-permute-start(f32[4,8,128]{2,1,0:T(8,128)S(1)} %get-tuple-element.26), channel_id=1, source_target_pairs={{0,6},{2,4},{4,2},{6,0},{8,14},{10,12},{12,10},{14,8},{16,22},{18,... | collective-permute-start | bytes 49160 | tf_op jit(solution)/shard_map/ppermute | solution.py:25
  27.1 5.9 %collective-permute-start.1 = (f32[4,64,128]{2,1,0:T(8,128)S(1)}, f32[4,64,128]{2,1,0:T(8,128)S(1)}, u32[]{:S(2)}, u32[]{:S(2)}) collective-permute-start(f32[4,64,128]{2,1,0:T(8,128)S(1)} %get-tuple-element.20), channel_id=1, source_target_pairs={{0,2},{2,0},{4,6},{6,4},{8,10},{10,8},{12,14},{14,12},{16,18},{18,... | collective-permute-start | bytes 393224 | tf_op jit(solution)/shard_map/ppermute | solution.py:25
  28.2 7.8 %collective-permute-start.2 = (f32[4,64,128]{2,1,0:T(8,128)S(1)}, f32[4,64,128]{2,1,0:T(8,128)S(1)}, u32[]{:S(2)}, u32[]{:S(2)}) collective-permute-start(f32[4,64,128]{2,1,0:T(8,128)S(1)} %get-tuple-element.22), channel_id=1, source_target_pairs={{0,4},{2,6},{4,0},{6,2},{8,12},{10,14},{12,8},{14,10},{16,20},{18,... | collective-permute-start | bytes 393224 | tf_op jit(solution)/shard_map/ppermute | solution.py:25
  29.7 6.2 %collective-permute-start.3 = (f32[4,64,128]{2,1,0:T(8,128)S(1)}, f32[4,64,128]{2,1,0:T(8,128)S(1)}, u32[]{:S(2)}, u32[]{:S(2)}) collective-permute-start(f32[4,64,128]{2,1,0:T(8,128)S(1)} %get-tuple-element.21), channel_id=1, source_target_pairs={{0,6},{2,4},{4,2},{6,0},{8,14},{10,12},{12,10},{14,8},{16,22},{18,... | collective-permute-start | bytes 393224 | tf_op jit(solution)/shard_map/ppermute | solution.py:25
  36.0 4.9 %collective-permute-start.9 = (f32[2,72,128]{2,1,0:T(8,128)S(1)}, f32[2,72,128]{2,1,0:T(8,128)S(1)}, u32[]{:S(2)}, u32[]{:S(2)}) collective-permute-start(f32[2,72,128]{2,1,0:T(8,128)S(1)} %pad_maximum_fusion), channel_id=1, source_target_pairs={{0,8},{2,10},{4,12},{6,14},{8,0},{10,2},{12,4},{14,6},{16,24},{18,... | collective-permute-start | bytes 221192 | tf_op jit(solution)/shard_map/ppermute | solution.py:25
  40.9 5.4 %collective-permute-start.10 = (f32[1,72,128]{2,1,0:T(8,128)S(1)}, f32[1,72,128]{2,1,0:T(8,128)S(1)}, u32[]{:S(2)}, u32[]{:S(2)}) collective-permute-start(f32[1,72,128]{2,1,0:T(8,128)S(1)} %get-tuple-element.23), channel_id=1, source_target_pairs={{0,16},{2,18},{4,20},{6,22},{8,24},{10,26},{12,28},{14,30},{16,0},... | collective-permute-start | bytes 110600 | tf_op jit(solution)/shard_map/ppermute | solution.py:25
  49.9 12.5 %all-to-all-start = ((f32[16,4,128]{2,1,0:T(4,128)}), f32[16,4,128]{2,1,0:T(4,128)S(1)}, u32[]{:S(2)}, u32[]{:S(2)}) async-start(f32[16,4,128]{2,1,0:T(4,128)} %get-tuple-element.18), calls=%async_computation | async-start | bytes 65536 | tf_op jit(solution)/shard_map/all_to_all | solution.py:347

commit v3 on v2

--- a/solution.py
+++ b/solution.py
@@ -11,7 +11,6 @@
 GRAM_UNROLL = 4
 GRAD_UNROLL = 8
 PACK_UNROLL = 4
-PANEL = 8
 VMEM_LIMIT = 20 << 20
 EXTRA = 8
 PLANE = 4
@@ -141,8 +140,8 @@
     tb_rows = tb_ref[...]
     back = vox - 1 - lax.broadcasted_iota(jnp.int32, (GROUP, vox), 1)
     up = GROUP - 1 - lax.broadcasted_iota(jnp.int32, (GROUP, vox), 0)
-    sub = lax.broadcasted_iota(jnp.int32, (GROUP, vox), 0)
-    zero = jnp.zeros((blk, vox), jnp.bfloat16)
+    lrow = lax.broadcasted_iota(jnp.int32, (2 * GROUP, 4 * blk), 0)
+    lslot = lax.broadcasted_iota(jnp.int32, (2 * GROUP, 4 * blk), 1) // blk
 
     def group(g, mis):
         base = pl.multiple_of(g * GROUP, GROUP)
@@ -154,12 +153,17 @@
             resid = 0.5 * (obs_ref[h, rows, :] + mirror) - calc_ref[h, rows, :]
             mis = mis + resid * resid
             resids.append(resid)
-        lhs = jnp.concatenate(resids, axis=1).astype(jnp.bfloat16)
-        lines = jnp.zeros((GROUP, vox), jnp.float32)
-        for u in range(GROUP):
-            grad = nt_dot(lhs, diagonal_pair(jbuf[0, base + u], jbuf[1, base + u], zero))
-            lines = jnp.where(sub == u, grad, lines)
-        tg[rows, :] = lines
+        none = jnp.zeros_like(resids[0])
+        lhs = jnp.concatenate(
+            [jnp.concatenate([resids[0], none], axis=0), jnp.concatenate([none, resids[1]], axis=0)], axis=1
+        ).astype(jnp.bfloat16)
+        lines = jnp.zeros((2 * GROUP, 4 * blk), jnp.float32)
+        for a in range(0, GROUP, 4):
+            four = [jbuf[h, pl.ds(base + a, 4)].reshape(4 * blk, vox) for h in range(2)]
+            out = nt_dot(lhs, jnp.concatenate(four, axis=1))
+            lines = jnp.where((lrow & 7) == a + lslot, out, lines)
+        tg[pl.ds(base, GROUP), :] = lines[:GROUP]
+        tg[pl.ds(pl.multiple_of(side_tiles + base, GROUP), GROUP), :] = lines[GROUP:]
         return mis
 
     mis = lax.fori_loop(0, side_tiles // GROUP, group, jnp.zeros((GROUP, vox), jnp.float32), unroll=GRAD_UNROLL)
@@ -168,19 +172,16 @@
     pairs = diag_ref.shape[2]
     total = jnp.sum(mis, axis=0, keepdims=True)
     rest = jnp.zeros((EXTRA - 2 * pairs - 1, vox), jnp.float32)
-    block = lax.broadcasted_iota(jnp.int32, (NB, side_tiles), 0)
-    sums = [
-        jnp.dot(
-            (block == tb_row).astype(jnp.float32),
-            tg[...],
-            precision=lax.Precision.HIGHEST,
-            preferred_element_type=jnp.float32,
-        )
-        for tb_row in (tb_rows[0:1], tb_rows[1:2])
-    ]
-    high = lax.broadcasted_iota(jnp.int32, sums[0].shape, 1) >= blk
-    odd = (lax.broadcasted_iota(jnp.int32, sums[0].shape, 0) % 2) == 1
-    own = jnp.where(high, sums[1], sums[0])
+    block = lax.broadcasted_iota(jnp.int32, (NB, 2 * side_tiles), 0)
+    own = jnp.dot(
+        (block == tb_rows).astype(jnp.float32),
+        tg[...],
+        precision=lax.Precision.HIGHEST,
+        preferred_element_type=jnp.float32,
+    )
+    own = own[:, : 2 * blk] + own[:, 2 * blk :]
+    high = lax.broadcasted_iota(jnp.int32, own.shape, 1) >= blk
+    odd = (lax.broadcasted_iota(jnp.int32, own.shape, 0) % 2) == 1
     mix[...] = jnp.where(odd == high, own + pltpu.roll(own, blk, 1), 0.0)
     for part, ref in enumerate((keep_ref, send_ref)):
         def chunk(c, carry, part=part, ref=ref):
@@ -242,26 +243,32 @@
     sub = lax.broadcasted_iota(jnp.int32, (8, width), 0)
     lanes = lax.broadcasted_iota(jnp.int32, (8, width), 1)
     side = lanes - lanes % blk
-    for k in range(0, blk, PANEL):
+    for k in range(0, blk, 8):
         own = k // 8
         for m, right in zip(mats, rights):
-            cols = [[gathered(m[i], side + (k + j), 1) for i in range(tall)] for j in range(PANEL)]
+            cols = [[gathered(m[i], side + (k + j), 1) for i in range(tall)] for j in range(8)]
+            held = [m] if k else [m, right]
+            done = [part[own] for part in held]
+            local = [col[own] for col in cols]
+            for j in range(8):
+                inverse = 1.0 / jnp.broadcast_to(local[j][j : j + 1], (8, width))
+
+                def eliminate(part):
+                    prow = jnp.broadcast_to(part[j : j + 1], (8, width)) * inverse
+                    return jnp.where(sub == j, prow, part - local[j] * prow)
+
+                local[j + 1 :] = [eliminate(part) for part in local[j + 1 :]]
+                done = [eliminate(part) for part in done]
+            for part, final in zip(held, done):
+                prows = [jnp.broadcast_to(final[j : j + 1], (8, width)) for j in range(8)]
+                for i in range(tall):
+                    if i == own:
+                        part[i] = final
+                    else:
+                        for j in range(8):
+                            part[i] = part[i] - cols[j][i] * prows[j]
             if k == 0:
-                cols.append(right)
-            for j in range(PANEL):
-                at = (k + j) % 8
-                pivot = jnp.broadcast_to(cols[j][own][at : at + 1], (8, width))
-
-                def eliminate(part):
-                    prow = jnp.broadcast_to(part[own][at : at + 1], (8, width)) / pivot
-                    new = [part[i] - cols[j][i] * prow for i in range(tall)]
-                    new[own] = jnp.where(sub == at, prow, new[own])
-                    return new
-
-                cols[j + 1 :] = [eliminate(col) for col in cols[j + 1 :]]
-                m[:] = eliminate(m)
-            if k == 0:
-                m[:] = [jnp.where(lanes == side, cols[PANEL][i], m[i]) for i in range(tall)]
+                m[:] = [jnp.where(lanes == side, right[i], m[i]) for i in range(tall)]
     lines = []
     for m, diag in zip(mats, diags):
         line = jnp.zeros((8, width), jnp.float32)
@@ -323,10 +330,10 @@
         out_shape=(extra, extra),
         in_specs=[vmem] * 6,
         out_specs=(vmem, vmem),
-        scratch_shapes=[pltpu.VMEM((side_tiles, vox), jnp.float32), pltpu.VMEM((NB, vox), jnp.float32)],
+        scratch_shapes=[pltpu.VMEM((tiles, 4 * blk), jnp.float32), pltpu.VMEM((NB, vox), jnp.float32)],
         compiler_params=limit,
         name="grad",
-    )(halved(tile_block), local(staged), local(calc), halved(observed), local(halved(moved)), local(diag))
+    )(tile_block[None], local(staged), local(calc), halved(observed), local(halved(moved)), local(diag))
     other = xored(send, "gy", 1)
     both = keep + other
     rest = plane(both)

time: 64.3 us -> 63 us (0.980)
  Pallas kernels: 13.9 us -> 12.5 us
    pallas_call x1, Pallas kernels: 3.23 us -> 2.09 us  [fast_inner(): pl.pallas_call(grad_body, out_shape=(extra, extra), in_specs=[vmem] * 6,...]
  transfers between devices with their start and end apart: 12 -> 12, of which waited for: 8 -> 8; matrix products, arithmetic and copies ran while one was open for 1% -> 1% of each run, Pallas kernels for 5% -> 3%
where the time goes in v3:
time: 63 us; the launch traced here: 62.7 us
  starting transfers between devices  25.5 us (40%)
  waiting for transfers between devices  20.2 us (32%)
  Pallas kernels  12.5 us (20%)
  between operations  3.16 us (5%)
  local copies, waits for them, and re-layouts  1.18 us (2%)
    ppermute x10, starting transfers between devices, xored(): lax.ppermute(value, axis, [(i, i ^ bit) for i in range(lax.axis_size(axis...  13.9 us
    ppermute x10, waiting for transfers between devices, xored(): lax.ppermute(value, axis, [(i, i ^ bit) for i in range(lax.axis_size(axis...  10.1 us
    pallas_call x1, Pallas kernels, fast_inner(): pl.pallas_call(gram_body, out_shape=(pltpu.VMEM((2, side_tiles, vox), jnp...  7.15 us
    ppermute x1, starting transfers between devices, flipped(): return lax.ppermute(value, axes, [(i, size - 1 - i) for i in range(size)])  6.58 us
    all_to_all x1, waiting for transfers between devices, fast_inner(): every = lax.all_to_all(step, 'gx', 0, 0)  6.24 us
    all_to_all x1, starting transfers between devices, fast_inner(): every = lax.all_to_all(step, 'gx', 0, 0)  5.06 us
    ppermute x1, waiting for transfers between devices, flipped(): return lax.ppermute(value, axes, [(i, size - 1 - i) for i in range(size)])  3.89 us
    pallas_call x1, Pallas kernels, fast_inner(): pl.pallas_call(solve_body, out_shape=(jax.ShapeDtypeStruct((ngx, per, vox...  3.29 us
  transfers between devices with their start and end apart: 12, of which 8 were waited for; matrix products, arithmetic and copies ran while one was open for 1% of the time, Pallas kernels for 3%

profile of v3, /device:TPU:0, one launch (start us, length us, event | category | flops | bytes accessed | tf_op | source)
XLA Modules:
  0.0 62.7 jit_solution(11576151570256531704)
XLA Ops:
  0.6 0.0 copy-start.1
  0.6 0.0 copy-start
  0.7 7.2 %gram.1 = (f32[2,128,128]{2,1,0:T(8,128)S(1)}, f32[16,64,128]{2,1,0:T(8,128)S(1)}, f32[16,64,128]{2,1,0:T(8,128)S(1)}, f32[2,16,2,128]{3,2,1,0:T(2,128)S(1)}, bf16[2,128,64,128]{3,2,1,0:T(8,128)(2,1)S(1)}) custom-call(s32[256]{0:T(256)} %tb.1, bf16[2,128,64,128]{3,2,1,0:T(8,128)(2,1)} %bitcast.11, f32[64,128]{1,0:T(8,128)} %bitcast.13), custom_call_target="tpu_custom_call" | custom-call | tf_op jit(solution)/shard_map/gram/pallas_call | solution.py:307
  7.8 0.6 collective-permute-start
  8.4 0.0 copy-done
  8.4 6.6 %collective-permute-start.4 = (f32[256,128]{1,0:T(8,128)S(1)}, f32[256,128]{1,0:T(8,128)S(1)}, u32[]{:S(2)}, u32[]{:S(2)}) collective-permute-start(f32[256,128]{1,0:T(8,128)S(1)} %copy-done), channel_id=1, source_target_pairs={{0,31},{1,30},{2,29},{3,28},{4,27},{5,26},{6,25},{7,24},{8,23},{9,... | collective-permute-start | bytes 393224 | tf_op jit(solution)/shard_map/ppermute | solution.py:20
  14.9 3.9 %collective-permute-done.4 = f32[256,128]{1,0:T(8,128)S(1)} collective-permute-done((f32[256,128]{1,0:T(8,128)S(1)}, f32[256,128]{1,0:T(8,128)S(1)}, u32[]{:S(2)}, u32[]{:S(2)}) %collective-permute-start.4) | collective-permute-done | bytes 131104 | tf_op jit(solution)/shard_map/ppermute | solution.py:20
  18.8 0.0 copy-done.1
  18.8 2.1 %grad.1 = (f32[16,8,128]{2,1,0:T(8,128)S(1)}, f32[16,8,128]{2,1,0:T(8,128)S(1)}) custom-call(s32[1,256]{1,0:T(1,128)S(1)} %bitcast.10, bf16[2,128,64,128]{3,2,1,0:T(8,128)(2,1)S(1)} %get-tuple-element.13.jbuf, f32[2,128,128]{2,1,0:T(8,128)S(1)} %get-tuple-element.14.calc_ref, f32[2,128,128]{2,1,0:T(8,128)S(1)} %bitcast.8, f32[2,128,128]{2,1,0:T(8,128)S(1)} %bitcast.9, ...), custom_call_target="tpu_custom_call" | custom-call | tf_op jit(solution)/shard_map/grad/pallas_call | solution.py:328
  20.9 0.2 collective-permute-start.5
  21.1 1.2 %collective-permute-done.5 = f32[16,8,128]{2,1,0:T(8,128)S(1)} collective-permute-done((f32[16,8,128]{2,1,0:T(8,128)S(1)}, f32[16,8,128]{2,1,0:T(8,128)S(1)}, u32[]{:S(2)}, u32[]{:S(2)}) %collective-permute-start.5) | collective-permute-done | bytes 65568 | tf_op jit(solution)/shard_map/ppermute | solution.py:24
  22.3 1.1 %collective-permute-start.6 = (f32[4,8,128]{2,1,0:T(8,128)S(1)}, f32[4,8,128]{2,1,0:T(8,128)S(1)}, u32[]{:S(2)}, u32[]{:S(2)}) collective-permute-start(f32[4,8,128]{2,1,0:T(8,128)S(1)} %get-tuple-element.25), channel_id=1, source_target_pairs={{0,2},{2,0},{4,6},{6,4},{8,10},{10,8},{12,14},{14,12},{16,18},{18,... | collective-permute-start | bytes 49160 | tf_op jit(solution)/shard_map/ppermute | solution.py:24
  23.4 1.5 %collective-permute-start.7 = (f32[4,8,128]{2,1,0:T(8,128)S(1)}, f32[4,8,128]{2,1,0:T(8,128)S(1)}, u32[]{:S(2)}, u32[]{:S(2)}) collective-permute-start(f32[4,8,128]{2,1,0:T(8,128)S(1)} %get-tuple-element.27), channel_id=1, source_target_pairs={{0,4},{2,6},{4,0},{6,2},{8,12},{10,14},{12,8},{14,10},{16,20},{18,... | collective-permute-start | bytes 49160 | tf_op jit(solution)/shard_map/ppermute | solution.py:24
  24.9 0.9 %collective-permute-start.8 = (f32[4,8,128]{2,1,0:T(8,128)S(1)}, f32[4,8,128]{2,1,0:T(8,128)S(1)}, u32[]{:S(2)}, u32[]{:S(2)}) collective-permute-start(f32[4,8,128]{2,1,0:T(8,128)S(1)} %get-tuple-element.26), channel_id=1, source_target_pairs={{0,6},{2,4},{4,2},{6,0},{8,14},{10,12},{12,10},{14,8},{16,22},{18,... | collective-permute-start | bytes 49160 | tf_op jit(solution)/shard_map/ppermute | solution.py:24
  25.8 0.0 collective-permute-done
  25.8 0.1 add.27
  25.9 1.1 %collective-permute-start.1 = (f32[4,64,128]{2,1,0:T(8,128)S(1)}, f32[4,64,128]{2,1,0:T(8,128)S(1)}, u32[]{:S(2)}, u32[]{:S(2)}) collective-permute-start(f32[4,64,128]{2,1,0:T(8,128)S(1)} %get-tuple-element.20), channel_id=1, source_target_pairs={{0,2},{2,0},{4,6},{6,4},{8,10},{10,8},{12,14},{14,12},{16,18},{18,... | collective-permute-start | bytes 393224 | tf_op jit(solution)/shard_map/ppermute | solution.py:24
  27.0 1.5 %collective-permute-start.2 = (f32[4,64,128]{2,1,0:T(8,128)S(1)}, f32[4,64,128]{2,1,0:T(8,128)S(1)}, u32[]{:S(2)}, u32[]{:S(2)}) collective-permute-start(f32[4,64,128]{2,1,0:T(8,128)S(1)} %get-tuple-element.22), channel_id=1, source_target_pairs={{0,4},{2,6},{4,0},{6,2},{8,12},{10,14},{12,8},{14,10},{16,20},{18,... | collective-permute-start | bytes 393224 | tf_op jit(solution)/shard_map/ppermute | solution.py:24
  28.6 0.0 collective-permute-done.6
  28.6 0.9 %collective-permute-start.3 = (f32[4,64,128]{2,1,0:T(8,128)S(1)}, f32[4,64,128]{2,1,0:T(8,128)S(1)}, u32[]{:S(2)}, u32[]{:S(2)}) collective-permute-start(f32[4,64,128]{2,1,0:T(8,128)S(1)} %get-tuple-element.21), channel_id=1, source_target_pairs={{0,6},{2,4},{4,2},{6,0},{8,14},{10,12},{12,10},{14,8},{16,22},{18,... | collective-permute-start | bytes 393224 | tf_op jit(solution)/shard_map/ppermute | solution.py:24
  29.5 0.0 collective-permute-done.7
  29.5 0.2 collective-permute-done.8
  29.7 2.1 %collective-permute-done.1 = f32[4,64,128]{2,1,0:T(8,128)S(1)} collective-permute-done((f32[4,64,128]{2,1,0:T(8,128)S(1)}, f32[4,64,128]{2,1,0:T(8,128)S(1)}, u32[]{:S(2)}, u32[]{:S(2)}) %collective-permute-start.1) | collective-permute-done | bytes 131104 | tf_op jit(solution)/shard_map/ppermute | solution.py:24
  31.9 3.0 %collective-permute-done.2 = f32[4,64,128]{2,1,0:T(8,128)S(1)} collective-permute-done((f32[4,64,128]{2,1,0:T(8,128)S(1)}, f32[4,64,128]{2,1,0:T(8,128)S(1)}, u32[]{:S(2)}, u32[]{:S(2)}) %collective-permute-start.2) | collective-permute-done | bytes 131104 | tf_op jit(solution)/shard_map/ppermute | solution.py:24
  34.8 0.0 collective-permute-done.3
  34.9 2.6 %collective-permute-start.9 = (f32[2,72,128]{2,1,0:T(8,128)S(1)}, f32[2,72,128]{2,1,0:T(8,128)S(1)}, u32[]{:S(2)}, u32[]{:S(2)}) collective-permute-start(f32[2,72,128]{2,1,0:T(8,128)S(1)} %pad_maximum_fusion), channel_id=1, source_target_pairs={{0,8},{2,10},{4,12},{6,14},{8,0},{10,2},{12,4},{14,6},{16,24},{18,... | collective-permute-start | bytes 221192 | tf_op jit(solution)/shard_map/ppermute | solution.py:24
  37.4 2.3 %collective-permute-done.9 = f32[2,72,128]{2,1,0:T(8,128)S(1)} collective-permute-done((f32[2,72,128]{2,1,0:T(8,128)S(1)}, f32[2,72,128]{2,1,0:T(8,128)S(1)}, u32[]{:S(2)}, u32[]{:S(2)}) %collective-permute-start.9) | collective-permute-done | bytes 73760 | tf_op jit(solution)/shard_map/ppermute | solution.py:24
  39.8 3.5 %collective-permute-start.10 = (f32[1,72,128]{2,1,0:T(8,128)S(1)}, f32[1,72,128]{2,1,0:T(8,128)S(1)}, u32[]{:S(2)}, u32[]{:S(2)}) collective-permute-start(f32[1,72,128]{2,1,0:T(8,128)S(1)} %get-tuple-element.23), channel_id=1, source_target_pairs={{0,16},{2,18},{4,20},{6,22},{8,24},{10,26},{12,28},{14,30},{16,0},... | collective-permute-start | bytes 110600 | tf_op jit(solution)/shard_map/ppermute | solution.py:24
  43.9 1.3 %collective-permute-done.10.b_ref = f32[1,72,128]{2,1,0:T(8,128)S(1)} collective-permute-done((f32[1,72,128]{2,1,0:T(8,128)S(1)}, f32[1,72,128]{2,1,0:T(8,128)S(1)}, u32[]{:S(2)}, u32[]{:S(2)}) %collective-permute-start.10) | collective-permute-done | bytes 36896 | tf_op jit(solution)/shard_map/ppermute | solution.py:24
  45.2 3.3 %solve.1 = (f32[16,4,128]{2,1,0:T(4,128)}, f32[8,128]{1,0:T(8,128)S(1)}) custom-call(f32[1]{0:T(128)S(6)} %copy.8.damp, f32[1,72,128]{2,1,0:T(8,128)S(1)} %get-tuple-element.24.a_ref, f32[1,72,128]{2,1,0:T(8,128)S(1)} %collective-permute-done.10.b_ref), custom_call_target="tpu_custom_call" | custom-call | tf_op jit(solution)/shard_map/solve/pallas_call | solution.py:346
  48.5 5.1 %all-to-all-start = ((f32[16,4,128]{2,1,0:T(4,128)}), f32[16,4,128]{2,1,0:T(4,128)S(1)}, u32[]{:S(2)}, u32[]{:S(2)}) async-start(f32[16,4,128]{2,1,0:T(4,128)} %get-tuple-element.18), calls=%async_computation | async-start | bytes 65536 | tf_op jit(solution)/shard_map/all_to_all | solution.py:354
  53.6 0.5 slice.63
  54.8 6.2 %all-to-all-done = f32[16,4,128]{2,1,0:T(4,128)S(1)} async-done(((f32[16,4,128]{2,1,0:T(4,128)}), f32[16,4,128]{2,1,0:T(4,128)S(1)}, u32[]{:S(2)}, u32[]{:S(2)}) %all-to-all-start) | async-done | bytes 32800 | tf_op jit(solution)/shard_map/all_to_all | solution.py:354
  61.0 0.6 copy.9
  (8 shorter events, 0.1 us)
Async XLA Ops:
  0.6 18.2 %copy-start.1 = (s32[256]{0:T(256)S(1)}, s32[256]{0:T(256)}, u32[]{:S(2)}) copy-start(s32[256]{0:T(256)} %tb.1) | copy-start | bytes 3076
  0.6 7.7 %copy-start = (f32[256,128]{1,0:T(8,128)S(1)}, f32[256,128]{1,0:T(8,128)}, u32[]{:S(2)}) copy-start(f32[256,128]{1,0:T(8,128)} %param.5) | copy-start | bytes 393220
  7.8 18.0 %collective-permute-start = (f32[16,64,128]{2,1,0:T(8,128)S(1)}, f32[16,64,128]{2,1,0:T(8,128)S(1)}, u32[]{:S(2)}, u32[]{:S(2)}) collective-permute-start(f32[16,64,128]{2,1,0:T(8,128)S(1)} %get-tuple-element.12), channel_id=1, source_target_pairs={{0,1},{1,0},{2,3},{3,2},{4,5},{5,4},{6,7},{7,6},{8,9},{9,8},{10,11... | collective-permute-start | bytes 1572872 | tf_op jit(solution)/shard_map/ppermute | solution.py:24
  8.4 10.5 %collective-permute-start.4 = (f32[256,128]{1,0:T(8,128)S(1)}, f32[256,128]{1,0:T(8,128)S(1)}, u32[]{:S(2)}, u32[]{:S(2)}) collective-permute-start(f32[256,128]{1,0:T(8,128)S(1)} %copy-done), channel_id=1, source_target_pairs={{0,31},{1,30},{2,29},{3,28},{4,27},{5,26},{6,25},{7,24},{8,23},{9,... | collective-permute-start | bytes 393224 | tf_op jit(solution)/shard_map/ppermute | solution.py:20
  20.9 1.3 %collective-permute-start.5 = (f32[16,8,128]{2,1,0:T(8,128)S(1)}, f32[16,8,128]{2,1,0:T(8,128)S(1)}, u32[]{:S(2)}, u32[]{:S(2)}) collective-permute-start(f32[16,8,128]{2,1,0:T(8,128)S(1)} %get-tuple-element.17), channel_id=1, source_target_pairs={{0,1},{1,0},{2,3},{3,2},{4,5},{5,4},{6,7},{7,6},{8,9},{9,8},{10,11... | collective-permute-start | bytes 196616 | tf_op jit(solution)/shard_map/ppermute | solution.py:24
  22.3 6.3 %collective-permute-start.6 = (f32[4,8,128]{2,1,0:T(8,128)S(1)}, f32[4,8,128]{2,1,0:T(8,128)S(1)}, u32[]{:S(2)}, u32[]{:S(2)}) collective-permute-start(f32[4,8,128]{2,1,0:T(8,128)S(1)} %get-tuple-element.25), channel_id=1, source_target_pairs={{0,2},{2,0},{4,6},{6,4},{8,10},{10,8},{12,14},{14,12},{16,18},{18,... | collective-permute-start | bytes 49160 | tf_op jit(solution)/shard_map/ppermute | solution.py:24
  23.4 6.1 %collective-permute-start.7 = (f32[4,8,128]{2,1,0:T(8,128)S(1)}, f32[4,8,128]{2,1,0:T(8,128)S(1)}, u32[]{:S(2)}, u32[]{:S(2)}) collective-permute-start(f32[4,8,128]{2,1,0:T(8,128)S(1)} %get-tuple-element.27), channel_id=1, source_target_pairs={{0,4},{2,6},{4,0},{6,2},{8,12},{10,14},{12,8},{14,10},{16,20},{18,... | collective-permute-start | bytes 49160 | tf_op jit(solution)/shard_map/ppermute | solution.py:24
  24.9 4.8 %collective-permute-start.8 = (f32[4,8,128]{2,1,0:T(8,128)S(1)}, f32[4,8,128]{2,1,0:T(8,128)S(1)}, u32[]{:S(2)}, u32[]{:S(2)}) collective-permute-start(f32[4,8,128]{2,1,0:T(8,128)S(1)} %get-tuple-element.26), channel_id=1, source_target_pairs={{0,6},{2,4},{4,2},{6,0},{8,14},{10,12},{12,10},{14,8},{16,22},{18,... | collective-permute-start | bytes 49160 | tf_op jit(solution)/shard_map/ppermute | solution.py:24
  25.9 5.9 %collective-permute-start.1 = (f32[4,64,128]{2,1,0:T(8,128)S(1)}, f32[4,64,128]{2,1,0:T(8,128)S(1)}, u32[]{:S(2)}, u32[]{:S(2)}) collective-permute-start(f32[4,64,128]{2,1,0:T(8,128)S(1)} %get-tuple-element.20), channel_id=1, source_target_pairs={{0,2},{2,0},{4,6},{6,4},{8,10},{10,8},{12,14},{14,12},{16,18},{18,... | collective-permute-start | bytes 393224 | tf_op jit(solution)/shard_map/ppermute | solution.py:24
  27.0 7.8 %collective-permute-start.2 = (f32[4,64,128]{2,1,0:T(8,128)S(1)}, f32[4,64,128]{2,1,0:T(8,128)S(1)}, u32[]{:S(2)}, u32[]{:S(2)}) collective-permute-start(f32[4,64,128]{2,1,0:T(8,128)S(1)} %get-tuple-element.22), channel_id=1, source_target_pairs={{0,4},{2,6},{4,0},{6,2},{8,12},{10,14},{12,8},{14,10},{16,20},{18,... | collective-permute-start | bytes 393224 | tf_op jit(solution)/shard_map/ppermute | solution.py:24
  28.6 6.3 %collective-permute-start.3 = (f32[4,64,128]{2,1,0:T(8,128)S(1)}, f32[4,64,128]{2,1,0:T(8,128)S(1)}, u32[]{:S(2)}, u32[]{:S(2)}) collective-permute-start(f32[4,64,128]{2,1,0:T(8,128)S(1)} %get-tuple-element.21), channel_id=1, source_target_pairs={{0,6},{2,4},{4,2},{6,0},{8,14},{10,12},{12,10},{14,8},{16,22},{18,... | collective-permute-start | bytes 393224 | tf_op jit(solution)/shard_map/ppermute | solution.py:24
  34.9 4.9 %collective-permute-start.9 = (f32[2,72,128]{2,1,0:T(8,128)S(1)}, f32[2,72,128]{2,1,0:T(8,128)S(1)}, u32[]{:S(2)}, u32[]{:S(2)}) collective-permute-start(f32[2,72,128]{2,1,0:T(8,128)S(1)} %pad_maximum_fusion), channel_id=1, source_target_pairs={{0,8},{2,10},{4,12},{6,14},{8,0},{10,2},{12,4},{14,6},{16,24},{18,... | collective-permute-start | bytes 221192 | tf_op jit(solution)/shard_map/ppermute | solution.py:24
  39.8 5.4 %collective-permute-start.10 = (f32[1,72,128]{2,1,0:T(8,128)S(1)}, f32[1,72,128]{2,1,0:T(8,128)S(1)}, u32[]{:S(2)}, u32[]{:S(2)}) collective-permute-start(f32[1,72,128]{2,1,0:T(8,128)S(1)} %get-tuple-element.23), channel_id=1, source_target_pairs={{0,16},{2,18},{4,20},{6,22},{8,24},{10,26},{12,28},{14,30},{16,0},... | collective-permute-start | bytes 110600 | tf_op jit(solution)/shard_map/ppermute | solution.py:24
  48.5 12.5 %all-to-all-start = ((f32[16,4,128]{2,1,0:T(4,128)}), f32[16,4,128]{2,1,0:T(4,128)S(1)}, u32[]{:S(2)}, u32[]{:S(2)}) async-start(f32[16,4,128]{2,1,0:T(4,128)} %get-tuple-element.18), calls=%async_computation | async-start | bytes 65536 | tf_op jit(solution)/shard_map/all_to_all | solution.py:354

commit v4 on v3

--- a/solution.py
+++ b/solution.py
@@ -9,7 +9,7 @@
 J_PARTS = 4
 GROUP = 8
 GRAM_UNROLL = 4
-GRAD_UNROLL = 8
+GRAD_UNROLL = 16
 PACK_UNROLL = 4
 VMEM_LIMIT = 20 << 20
 EXTRA = 8
@@ -129,13 +129,13 @@
                     jnp.where(use_top, cross[:half], cross[half:]), blk, 1
                 )
                 lines = [jnp.sum(jnp.where(on_diag, v, 0.0), axis=0, keepdims=True) for v in (stay, cross)]
-                diag_ref[part, c, p : p + 1, :] = lines[0] + pltpu.roll(lines[1], blk, 1)
+                diag_ref[part, c, pairs + p : pairs + p + 1, :] = lines[0] + pltpu.roll(lines[1], blk, 1)
             return carry
 
         lax.fori_loop(0, chunks, chunk, 0, unroll=PACK_UNROLL)
 
 
-def grad_body(tb_ref, jbuf, calc_ref, obs_ref, mir_ref, diag_ref, keep_ref, send_ref, tg, mix):
+def grad_body(tb_ref, jbuf, calc_ref, obs_ref, mir_ref, diag_ref, keep_ref, send_ref, tg, mix, paired):
     side_tiles, blk, vox = jbuf.shape[1:]
     tb_rows = tb_ref[...]
     back = vox - 1 - lax.broadcasted_iota(jnp.int32, (GROUP, vox), 1)
@@ -162,6 +162,7 @@
             four = [jbuf[h, pl.ds(base + a, 4)].reshape(4 * blk, vox) for h in range(2)]
             out = nt_dot(lhs, jnp.concatenate(four, axis=1))
             lines = jnp.where((lrow & 7) == a + lslot, out, lines)
+        lines = lines[:, : 2 * blk] + lines[:, 2 * blk :]
         tg[pl.ds(base, GROUP), :] = lines[:GROUP]
         tg[pl.ds(pl.multiple_of(side_tiles + base, GROUP), GROUP), :] = lines[GROUP:]
         return mis
@@ -169,28 +170,26 @@
     mis = lax.fori_loop(0, side_tiles // GROUP, group, jnp.zeros((GROUP, vox), jnp.float32), unroll=GRAD_UNROLL)
 
     chunks = keep_ref.shape[0]
-    pairs = diag_ref.shape[2]
+    pairs = NB // (4 * chunks)
     total = jnp.sum(mis, axis=0, keepdims=True)
-    rest = jnp.zeros((EXTRA - 2 * pairs - 1, vox), jnp.float32)
+    sub = lax.broadcasted_iota(jnp.int32, (EXTRA, vox), 0)
     block = lax.broadcasted_iota(jnp.int32, (NB, 2 * side_tiles), 0)
-    own = jnp.dot(
-        (block == tb_rows).astype(jnp.float32),
-        tg[...],
-        precision=lax.Precision.HIGHEST,
-        preferred_element_type=jnp.float32,
-    )
-    own = own[:, : 2 * blk] + own[:, 2 * blk :]
+    onehot = (block == tb_rows).astype(jnp.float32).astype(jnp.bfloat16)
+    left_over = tg[...]
+    own = jnp.zeros((NB, 2 * blk), jnp.float32)
+    for _ in range(3):
+        piece = left_over.astype(jnp.bfloat16)
+        left_over = left_over - piece.astype(jnp.float32)
+        own = own + jnp.dot(onehot, piece, preferred_element_type=jnp.float32)
     high = lax.broadcasted_iota(jnp.int32, own.shape, 1) >= blk
     odd = (lax.broadcasted_iota(jnp.int32, own.shape, 0) % 2) == 1
     mix[...] = jnp.where(odd == high, own + pltpu.roll(own, blk, 1), 0.0)
+    paired[...] = mix[pl.ds(0, NB // 2, stride=2), :] + mix[pl.ds(1, NB // 2, stride=2), :]
     for part, ref in enumerate((keep_ref, send_ref)):
-        def chunk(c, carry, part=part, ref=ref):
-            first = first_block(part, c, chunks, 2 * pairs)
-            rows = [mix[pl.ds(first + 2 * p, 1), :] + mix[pl.ds(first + 2 * p + 1, 1), :] for p in range(pairs)]
-            ref[c] = jnp.concatenate(rows + [diag_ref[part, c], total, rest], axis=0)
-            return carry
-
-        lax.fori_loop(0, chunks, chunk, 0, unroll=PACK_UNROLL)
+        for c in range(chunks):
+            tile = jnp.where(sub == 2 * pairs, total, jnp.where(sub < 2 * pairs, diag_ref[part, c], 0.0))
+            ref[c] = tile
+            ref[c, :pairs, :] = paired[pl.ds(first_block(part, c, chunks, 2 * pairs) // 2, pairs), :]
 
 
 def solve_body(damp, a_ref, b_ref, out_ref, mis_ref):
@@ -310,7 +309,7 @@
             pltpu.VMEM((2, side_tiles, vox), jnp.float32),
             payload,
             payload,
-            pltpu.VMEM((2, ngx, pairs, vox), jnp.float32),
+            pltpu.VMEM((2, ngx, EXTRA, vox), jnp.float32),
             pltpu.VMEM((2, side_tiles, blk, vox), jnp.bfloat16),
         ),
         in_specs=[smem, hbm, vmem],
@@ -330,7 +329,11 @@
         out_shape=(extra, extra),
         in_specs=[vmem] * 6,
         out_specs=(vmem, vmem),
-        scratch_shapes=[pltpu.VMEM((tiles, 4 * blk), jnp.float32), pltpu.VMEM((NB, vox), jnp.float32)],
+        scratch_shapes=[
+            pltpu.VMEM((tiles, 2 * blk), jnp.float32),
+            pltpu.VMEM((NB, vox), jnp.float32),
+            pltpu.VMEM((NB // 2, vox), jnp.float32),
+        ],
         compiler_params=limit,
         name="grad",
     )(tile_block[None], local(staged), local(calc), halved(observed), local(halved(moved)), local(diag))

time: 63 us -> 62.5 us (level)
  no operation moved by 1% of the time
where the time goes in v4:
time: 62.5 us; the launch traced here: 62.2 us
  starting transfers between devices  25.5 us (41%)
  waiting for transfers between devices  20.2 us (32%)
  Pallas kernels  12 us (19%)
  between operations  3.16 us (5%)
  local copies, waits for them, and re-layouts  1.18 us (2%)
    ppermute x10, starting transfers between devices, xored(): lax.ppermute(value, axis, [(i, i ^ bit) for i in range(lax.axis_size(axis...  13.9 us
    ppermute x10, waiting for transfers between devices, xored(): lax.ppermute(value, axis, [(i, i ^ bit) for i in range(lax.axis_size(axis...  10.1 us
    pallas_call x1, Pallas kernels, fast_inner(): pl.pallas_call(gram_body, out_shape=(pltpu.VMEM((2, side_tiles, vox), jnp...  7.15 us
    ppermute x1, starting transfers between devices, flipped(): return lax.ppermute(value, axes, [(i, size - 1 - i) for i in range(size)])  6.58 us
    all_to_all x1, waiting for transfers between devices, fast_inner(): every = lax.all_to_all(step, 'gx', 0, 0)  6.24 us
    all_to_all x1, starting transfers between devices, fast_inner(): every = lax.all_to_all(step, 'gx', 0, 0)  5.06 us
    ppermute x1, waiting for transfers between devices, flipped(): return lax.ppermute(value, axes, [(i, size - 1 - i) for i in range(size)])  3.89 us
    pallas_call x1, Pallas kernels, fast_inner(): pl.pallas_call(solve_body, out_shape=(jax.ShapeDtypeStruct((ngx, per, vox...  3.29 us
  transfers between devices with their start and end apart: 12, of which 8 were waited for; matrix products, arithmetic and copies ran while one was open for 1% of the time, Pallas kernels for 3%

profile of v4, /device:TPU:0, one launch (start us, length us, event | category | flops | bytes accessed | tf_op | source)
XLA Modules:
  0.0 62.2 jit_solution(5686605306544448515)
XLA Ops:
  0.6 0.0 copy-start.1
  0.6 0.0 copy-start
  0.7 7.2 %gram.1 = (f32[2,128,128]{2,1,0:T(8,128)S(1)}, f32[16,64,128]{2,1,0:T(8,128)S(1)}, f32[16,64,128]{2,1,0:T(8,128)S(1)}, f32[2,16,8,128]{3,2,1,0:T(8,128)S(1)}, bf16[2,128,64,128]{3,2,1,0:T(8,128)(2,1)S(1)}) custom-call(s32[256]{0:T(256)} %tb.1, bf16[2,128,64,128]{3,2,1,0:T(8,128)(2,1)} %bitcast.11, f32[64,128]{1,0:T(8,128)} %bitcast.13), custom_call_target="tpu_custom_call" | custom-call | tf_op jit(solution)/shard_map/gram/pallas_call | solution.py:306
  7.8 0.6 collective-permute-start
  8.4 0.0 copy-done
  8.4 6.6 %collective-permute-start.4 = (f32[256,128]{1,0:T(8,128)S(1)}, f32[256,128]{1,0:T(8,128)S(1)}, u32[]{:S(2)}, u32[]{:S(2)}) collective-permute-start(f32[256,128]{1,0:T(8,128)S(1)} %copy-done), channel_id=1, source_target_pairs={{0,31},{1,30},{2,29},{3,28},{4,27},{5,26},{6,25},{7,24},{8,23},{9,... | collective-permute-start | bytes 393224 | tf_op jit(solution)/shard_map/ppermute | solution.py:20
  14.9 3.9 %collective-permute-done.4 = f32[256,128]{1,0:T(8,128)S(1)} collective-permute-done((f32[256,128]{1,0:T(8,128)S(1)}, f32[256,128]{1,0:T(8,128)S(1)}, u32[]{:S(2)}, u32[]{:S(2)}) %collective-permute-start.4) | collective-permute-done | bytes 131104 | tf_op jit(solution)/shard_map/ppermute | solution.py:20
  18.8 0.0 copy-done.1
  18.8 1.6 %grad.1 = (f32[16,8,128]{2,1,0:T(8,128)S(1)}, f32[16,8,128]{2,1,0:T(8,128)S(1)}) custom-call(s32[1,256]{1,0:T(1,128)S(1)} %bitcast.10, bf16[2,128,64,128]{3,2,1,0:T(8,128)(2,1)S(1)} %get-tuple-element.13.jbuf, f32[2,128,128]{2,1,0:T(8,128)S(1)} %get-tuple-element.14.calc_ref, f32[2,128,128]{2,1,0:T(8,128)S(1)} %bitcast.8, f32[2,128,128]{2,1,0:T(8,128)S(1)} %bitcast.9, ...), custom_call_target="tpu_custom_call" | custom-call | tf_op jit(solution)/shard_map/grad/pallas_call | solution.py:327
  20.4 0.2 collective-permute-start.5
  20.6 1.2 %collective-permute-done.5 = f32[16,8,128]{2,1,0:T(8,128)S(1)} collective-permute-done((f32[16,8,128]{2,1,0:T(8,128)S(1)}, f32[16,8,128]{2,1,0:T(8,128)S(1)}, u32[]{:S(2)}, u32[]{:S(2)}) %collective-permute-start.5) | collective-permute-done | bytes 65568 | tf_op jit(solution)/shard_map/ppermute | solution.py:24
  21.8 1.1 %collective-permute-start.6 = (f32[4,8,128]{2,1,0:T(8,128)S(1)}, f32[4,8,128]{2,1,0:T(8,128)S(1)}, u32[]{:S(2)}, u32[]{:S(2)}) collective-permute-start(f32[4,8,128]{2,1,0:T(8,128)S(1)} %get-tuple-element.25), channel_id=1, source_target_pairs={{0,2},{2,0},{4,6},{6,4},{8,10},{10,8},{12,14},{14,12},{16,18},{18,... | collective-permute-start | bytes 49160 | tf_op jit(solution)/shard_map/ppermute | solution.py:24
  22.9 1.5 %collective-permute-start.7 = (f32[4,8,128]{2,1,0:T(8,128)S(1)}, f32[4,8,128]{2,1,0:T(8,128)S(1)}, u32[]{:S(2)}, u32[]{:S(2)}) collective-permute-start(f32[4,8,128]{2,1,0:T(8,128)S(1)} %get-tuple-element.27), channel_id=1, source_target_pairs={{0,4},{2,6},{4,0},{6,2},{8,12},{10,14},{12,8},{14,10},{16,20},{18,... | collective-permute-start | bytes 49160 | tf_op jit(solution)/shard_map/ppermute | solution.py:24
  24.4 0.9 %collective-permute-start.8 = (f32[4,8,128]{2,1,0:T(8,128)S(1)}, f32[4,8,128]{2,1,0:T(8,128)S(1)}, u32[]{:S(2)}, u32[]{:S(2)}) collective-permute-start(f32[4,8,128]{2,1,0:T(8,128)S(1)} %get-tuple-element.26), channel_id=1, source_target_pairs={{0,6},{2,4},{4,2},{6,0},{8,14},{10,12},{12,10},{14,8},{16,22},{18,... | collective-permute-start | bytes 49160 | tf_op jit(solution)/shard_map/ppermute | solution.py:24
  25.3 0.0 collective-permute-done
  25.3 0.1 add.27
  25.4 1.1 %collective-permute-start.1 = (f32[4,64,128]{2,1,0:T(8,128)S(1)}, f32[4,64,128]{2,1,0:T(8,128)S(1)}, u32[]{:S(2)}, u32[]{:S(2)}) collective-permute-start(f32[4,64,128]{2,1,0:T(8,128)S(1)} %get-tuple-element.20), channel_id=1, source_target_pairs={{0,2},{2,0},{4,6},{6,4},{8,10},{10,8},{12,14},{14,12},{16,18},{18,... | collective-permute-start | bytes 393224 | tf_op jit(solution)/shard_map/ppermute | solution.py:24
  26.5 1.5 %collective-permute-start.2 = (f32[4,64,128]{2,1,0:T(8,128)S(1)}, f32[4,64,128]{2,1,0:T(8,128)S(1)}, u32[]{:S(2)}, u32[]{:S(2)}) collective-permute-start(f32[4,64,128]{2,1,0:T(8,128)S(1)} %get-tuple-element.22), channel_id=1, source_target_pairs={{0,4},{2,6},{4,0},{6,2},{8,12},{10,14},{12,8},{14,10},{16,20},{18,... | collective-permute-start | bytes 393224 | tf_op jit(solution)/shard_map/ppermute | solution.py:24
  28.1 0.0 collective-permute-done.6
  28.1 0.9 %collective-permute-start.3 = (f32[4,64,128]{2,1,0:T(8,128)S(1)}, f32[4,64,128]{2,1,0:T(8,128)S(1)}, u32[]{:S(2)}, u32[]{:S(2)}) collective-permute-start(f32[4,64,128]{2,1,0:T(8,128)S(1)} %get-tuple-element.21), channel_id=1, source_target_pairs={{0,6},{2,4},{4,2},{6,0},{8,14},{10,12},{12,10},{14,8},{16,22},{18,... | collective-permute-start | bytes 393224 | tf_op jit(solution)/shard_map/ppermute | solution.py:24
  29.0 0.0 collective-permute-done.7
  29.0 0.2 collective-permute-done.8
  29.2 2.1 %collective-permute-done.1 = f32[4,64,128]{2,1,0:T(8,128)S(1)} collective-permute-done((f32[4,64,128]{2,1,0:T(8,128)S(1)}, f32[4,64,128]{2,1,0:T(8,128)S(1)}, u32[]{:S(2)}, u32[]{:S(2)}) %collective-permute-start.1) | collective-permute-done | bytes 131104 | tf_op jit(solution)/shard_map/ppermute | solution.py:24
  31.3 3.0 %collective-permute-done.2 = f32[4,64,128]{2,1,0:T(8,128)S(1)} collective-permute-done((f32[4,64,128]{2,1,0:T(8,128)S(1)}, f32[4,64,128]{2,1,0:T(8,128)S(1)}, u32[]{:S(2)}, u32[]{:S(2)}) %collective-permute-start.2) | collective-permute-done | bytes 131104 | tf_op jit(solution)/shard_map/ppermute | solution.py:24
  34.3 0.0 collective-permute-done.3
  34.4 2.5 %collective-permute-start.9 = (f32[2,72,128]{2,1,0:T(8,128)S(1)}, f32[2,72,128]{2,1,0:T(8,128)S(1)}, u32[]{:S(2)}, u32[]{:S(2)}) collective-permute-start(f32[2,72,128]{2,1,0:T(8,128)S(1)} %pad_maximum_fusion), channel_id=1, source_target_pairs={{0,8},{2,10},{4,12},{6,14},{8,0},{10,2},{12,4},{14,6},{16,24},{18,... | collective-permute-start | bytes 221192 | tf_op jit(solution)/shard_map/ppermute | solution.py:24
  36.9 2.3 %collective-permute-done.9 = f32[2,72,128]{2,1,0:T(8,128)S(1)} collective-permute-done((f32[2,72,128]{2,1,0:T(8,128)S(1)}, f32[2,72,128]{2,1,0:T(8,128)S(1)}, u32[]{:S(2)}, u32[]{:S(2)}) %collective-permute-start.9) | collective-permute-done | bytes 73760 | tf_op jit(solution)/shard_map/ppermute | solution.py:24
  39.3 3.5 %collective-permute-start.10 = (f32[1,72,128]{2,1,0:T(8,128)S(1)}, f32[1,72,128]{2,1,0:T(8,128)S(1)}, u32[]{:S(2)}, u32[]{:S(2)}) collective-permute-start(f32[1,72,128]{2,1,0:T(8,128)S(1)} %get-tuple-element.23), channel_id=1, source_target_pairs={{0,16},{2,18},{4,20},{6,22},{8,24},{10,26},{12,28},{14,30},{16,0},... | collective-permute-start | bytes 110600 | tf_op jit(solution)/shard_map/ppermute | solution.py:24
  43.4 1.3 %collective-permute-done.10.b_ref = f32[1,72,128]{2,1,0:T(8,128)S(1)} collective-permute-done((f32[1,72,128]{2,1,0:T(8,128)S(1)}, f32[1,72,128]{2,1,0:T(8,128)S(1)}, u32[]{:S(2)}, u32[]{:S(2)}) %collective-permute-start.10) | collective-permute-done | bytes 36896 | tf_op jit(solution)/shard_map/ppermute | solution.py:24
  44.7 3.3 %solve.1 = (f32[16,4,128]{2,1,0:T(4,128)}, f32[8,128]{1,0:T(8,128)S(1)}) custom-call(f32[1]{0:T(128)S(6)} %copy.8.damp, f32[1,72,128]{2,1,0:T(8,128)S(1)} %get-tuple-element.24.a_ref, f32[1,72,128]{2,1,0:T(8,128)S(1)} %collective-permute-done.10.b_ref), custom_call_target="tpu_custom_call" | custom-call | tf_op jit(solution)/shard_map/solve/pallas_call | solution.py:349
  48.0 5.1 %all-to-all-start = ((f32[16,4,128]{2,1,0:T(4,128)}), f32[16,4,128]{2,1,0:T(4,128)S(1)}, u32[]{:S(2)}, u32[]{:S(2)}) async-start(f32[16,4,128]{2,1,0:T(4,128)} %get-tuple-element.18), calls=%async_computation | async-start | bytes 65536 | tf_op jit(solution)/shard_map/all_to_all | solution.py:357
  53.1 0.5 slice.63
  54.2 6.2 %all-to-all-done = f32[16,4,128]{2,1,0:T(4,128)S(1)} async-done(((f32[16,4,128]{2,1,0:T(4,128)}), f32[16,4,128]{2,1,0:T(4,128)S(1)}, u32[]{:S(2)}, u32[]{:S(2)}) %all-to-all-start) | async-done | bytes 32800 | tf_op jit(solution)/shard_map/all_to_all | solution.py:357
  60.5 0.6 copy.9
  (8 shorter events, 0.1 us)
Async XLA Ops:
  0.6 18.2 %copy-start.1 = (s32[256]{0:T(256)S(1)}, s32[256]{0:T(256)}, u32[]{:S(2)}) copy-start(s32[256]{0:T(256)} %tb.1) | copy-start | bytes 3076
  0.6 7.7 %copy-start = (f32[256,128]{1,0:T(8,128)S(1)}, f32[256,128]{1,0:T(8,128)}, u32[]{:S(2)}) copy-start(f32[256,128]{1,0:T(8,128)} %param.5) | copy-start | bytes 393220
  7.8 17.5 %collective-permute-start = (f32[16,64,128]{2,1,0:T(8,128)S(1)}, f32[16,64,128]{2,1,0:T(8,128)S(1)}, u32[]{:S(2)}, u32[]{:S(2)}) collective-permute-start(f32[16,64,128]{2,1,0:T(8,128)S(1)} %get-tuple-element.12), channel_id=1, source_target_pairs={{0,1},{1,0},{2,3},{3,2},{4,5},{5,4},{6,7},{7,6},{8,9},{9,8},{10,11... | collective-permute-start | bytes 1572872 | tf_op jit(solution)/shard_map/ppermute | solution.py:24
  8.4 10.5 %collective-permute-start.4 = (f32[256,128]{1,0:T(8,128)S(1)}, f32[256,128]{1,0:T(8,128)S(1)}, u32[]{:S(2)}, u32[]{:S(2)}) collective-permute-start(f32[256,128]{1,0:T(8,128)S(1)} %copy-done), channel_id=1, source_target_pairs={{0,31},{1,30},{2,29},{3,28},{4,27},{5,26},{6,25},{7,24},{8,23},{9,... | collective-permute-start | bytes 393224 | tf_op jit(solution)/shard_map/ppermute | solution.py:20
  20.4 1.3 %collective-permute-start.5 = (f32[16,8,128]{2,1,0:T(8,128)S(1)}, f32[16,8,128]{2,1,0:T(8,128)S(1)}, u32[]{:S(2)}, u32[]{:S(2)}) collective-permute-start(f32[16,8,128]{2,1,0:T(8,128)S(1)} %get-tuple-element.17), channel_id=1, source_target_pairs={{0,1},{1,0},{2,3},{3,2},{4,5},{5,4},{6,7},{7,6},{8,9},{9,8},{10,11... | collective-permute-start | bytes 196616 | tf_op jit(solution)/shard_map/ppermute | solution.py:24
  21.8 6.3 %collective-permute-start.6 = (f32[4,8,128]{2,1,0:T(8,128)S(1)}, f32[4,8,128]{2,1,0:T(8,128)S(1)}, u32[]{:S(2)}, u32[]{:S(2)}) collective-permute-start(f32[4,8,128]{2,1,0:T(8,128)S(1)} %get-tuple-element.25), channel_id=1, source_target_pairs={{0,2},{2,0},{4,6},{6,4},{8,10},{10,8},{12,14},{14,12},{16,18},{18,... | collective-permute-start | bytes 49160 | tf_op jit(solution)/shard_map/ppermute | solution.py:24
  22.9 6.1 %collective-permute-start.7 = (f32[4,8,128]{2,1,0:T(8,128)S(1)}, f32[4,8,128]{2,1,0:T(8,128)S(1)}, u32[]{:S(2)}, u32[]{:S(2)}) collective-permute-start(f32[4,8,128]{2,1,0:T(8,128)S(1)} %get-tuple-element.27), channel_id=1, source_target_pairs={{0,4},{2,6},{4,0},{6,2},{8,12},{10,14},{12,8},{14,10},{16,20},{18,... | collective-permute-start | bytes 49160 | tf_op jit(solution)/shard_map/ppermute | solution.py:24
  24.4 4.8 %collective-permute-start.8 = (f32[4,8,128]{2,1,0:T(8,128)S(1)}, f32[4,8,128]{2,1,0:T(8,128)S(1)}, u32[]{:S(2)}, u32[]{:S(2)}) collective-permute-start(f32[4,8,128]{2,1,0:T(8,128)S(1)} %get-tuple-element.26), channel_id=1, source_target_pairs={{0,6},{2,4},{4,2},{6,0},{8,14},{10,12},{12,10},{14,8},{16,22},{18,... | collective-permute-start | bytes 49160 | tf_op jit(solution)/shard_map/ppermute | solution.py:24
  25.4 5.9 %collective-permute-start.1 = (f32[4,64,128]{2,1,0:T(8,128)S(1)}, f32[4,64,128]{2,1,0:T(8,128)S(1)}, u32[]{:S(2)}, u32[]{:S(2)}) collective-permute-start(f32[4,64,128]{2,1,0:T(8,128)S(1)} %get-tuple-element.20), channel_id=1, source_target_pairs={{0,2},{2,0},{4,6},{6,4},{8,10},{10,8},{12,14},{14,12},{16,18},{18,... | collective-permute-start | bytes 393224 | tf_op jit(solution)/shard_map/ppermute | solution.py:24
  26.5 7.8 %collective-permute-start.2 = (f32[4,64,128]{2,1,0:T(8,128)S(1)}, f32[4,64,128]{2,1,0:T(8,128)S(1)}, u32[]{:S(2)}, u32[]{:S(2)}) collective-permute-start(f32[4,64,128]{2,1,0:T(8,128)S(1)} %get-tuple-element.22), channel_id=1, source_target_pairs={{0,4},{2,6},{4,0},{6,2},{8,12},{10,14},{12,8},{14,10},{16,20},{18,... | collective-permute-start | bytes 393224 | tf_op jit(solution)/shard_map/ppermute | solution.py:24
  28.1 6.3 %collective-permute-start.3 = (f32[4,64,128]{2,1,0:T(8,128)S(1)}, f32[4,64,128]{2,1,0:T(8,128)S(1)}, u32[]{:S(2)}, u32[]{:S(2)}) collective-permute-start(f32[4,64,128]{2,1,0:T(8,128)S(1)} %get-tuple-element.21), channel_id=1, source_target_pairs={{0,6},{2,4},{4,2},{6,0},{8,14},{10,12},{12,10},{14,8},{16,22},{18,... | collective-permute-start | bytes 393224 | tf_op jit(solution)/shard_map/ppermute | solution.py:24
  34.4 4.9 %collective-permute-start.9 = (f32[2,72,128]{2,1,0:T(8,128)S(1)}, f32[2,72,128]{2,1,0:T(8,128)S(1)}, u32[]{:S(2)}, u32[]{:S(2)}) collective-permute-start(f32[2,72,128]{2,1,0:T(8,128)S(1)} %pad_maximum_fusion), channel_id=1, source_target_pairs={{0,8},{2,10},{4,12},{6,14},{8,0},{10,2},{12,4},{14,6},{16,24},{18,... | collective-permute-start | bytes 221192 | tf_op jit(solution)/shard_map/ppermute | solution.py:24
  39.3 5.4 %collective-permute-start.10 = (f32[1,72,128]{2,1,0:T(8,128)S(1)}, f32[1,72,128]{2,1,0:T(8,128)S(1)}, u32[]{:S(2)}, u32[]{:S(2)}) collective-permute-start(f32[1,72,128]{2,1,0:T(8,128)S(1)} %get-tuple-element.23), channel_id=1, source_target_pairs={{0,16},{2,18},{4,20},{6,22},{8,24},{10,26},{12,28},{14,30},{16,0},... | collective-permute-start | bytes 110600 | tf_op jit(solution)/shard_map/ppermute | solution.py:24
  48.0 12.5 %all-to-all-start = ((f32[16,4,128]{2,1,0:T(4,128)}), f32[16,4,128]{2,1,0:T(4,128)S(1)}, u32[]{:S(2)}, u32[]{:S(2)}) async-start(f32[16,4,128]{2,1,0:T(4,128)} %get-tuple-element.18), calls=%async_computation | async-start | bytes 65536 | tf_op jit(solution)/shard_map/all_to_all | solution.py:357

commit v5 on v4

--- a/solution.py
+++ b/solution.py
@@ -10,8 +10,8 @@
 GROUP = 8
 GRAM_UNROLL = 4
 GRAD_UNROLL = 16
-PACK_UNROLL = 4
-VMEM_LIMIT = 20 << 20
+PACK_UNROLL = 8
+VMEM_LIMIT = 16 << 20
 EXTRA = 8
 PLANE = 4
 
@@ -75,7 +75,7 @@
     side_tiles, blk, vox = jbuf.shape[1:]
     half = blk // 2
     acc[...] = jnp.zeros_like(acc)
-    par[...] = jnp.concatenate([par_ref[...], par_ref[...]], axis=0).T.astype(jnp.bfloat16).astype(jnp.float32)
+    par[:NB, :] = jnp.concatenate([par_ref[...], par_ref[...]], axis=0).T.astype(jnp.bfloat16).astype(jnp.float32)
     zero = jnp.zeros((blk, vox), jnp.bfloat16)
     low = lax.broadcasted_iota(jnp.int32, (blk, 2 * blk), 1) < blk
     high = jnp.logical_not(low)
@@ -183,8 +183,8 @@
         own = own + jnp.dot(onehot, piece, preferred_element_type=jnp.float32)
     high = lax.broadcasted_iota(jnp.int32, own.shape, 1) >= blk
     odd = (lax.broadcasted_iota(jnp.int32, own.shape, 0) % 2) == 1
-    mix[...] = jnp.where(odd == high, own + pltpu.roll(own, blk, 1), 0.0)
-    paired[...] = mix[pl.ds(0, NB // 2, stride=2), :] + mix[pl.ds(1, NB // 2, stride=2), :]
+    mix[:NB, :] = jnp.where(odd == high, own + pltpu.roll(own, blk, 1), 0.0)
+    paired[: NB // 2, :] = mix[pl.ds(0, NB // 2, stride=2), :] + mix[pl.ds(1, NB // 2, stride=2), :]
     for part, ref in enumerate((keep_ref, send_ref)):
         for c in range(chunks):
             tile = jnp.where(sub == 2 * pairs, total, jnp.where(sub < 2 * pairs, diag_ref[part, c], 0.0))
@@ -316,7 +316,7 @@
         out_specs=(vmem, vmem, vmem, vmem, vmem),
         scratch_shapes=[
             pltpu.VMEM((NB, blk, 2 * blk), jnp.float32),
-            pltpu.VMEM((NB, 2 * blk), jnp.float32),
+            pltpu.VMEM((NB + GROUP, 2 * blk), jnp.float32),
             pltpu.SemaphoreType.DMA((J_PARTS,)),
         ],
         compiler_params=limit,
@@ -331,8 +331,8 @@
         out_specs=(vmem, vmem),
         scratch_shapes=[
             pltpu.VMEM((tiles, 2 * blk), jnp.float32),
-            pltpu.VMEM((NB, vox), jnp.float32),
-            pltpu.VMEM((NB // 2, vox), jnp.float32),
+            pltpu.VMEM((NB + GROUP, vox), jnp.float32),
+            pltpu.VMEM((NB // 2 + GROUP, vox), jnp.float32),
         ],
         compiler_params=limit,
         name="grad",

time: 62.5 us -> 62.1 us (level)
  no operation moved by 1% of the time
where the time goes in v5:
time: 62.1 us; the launch traced here: 61.9 us
  starting transfers between devices  25.5 us (41%)
  waiting for transfers between devices  20.2 us (33%)
  Pallas kernels  11.7 us (19%)
  between operations  3.16 us (5%)
  local copies, waits for them, and re-layouts  1.18 us (2%)
    ppermute x10, starting transfers between devices, xored(): lax.ppermute(value, axis, [(i, i ^ bit) for i in range(lax.axis_size(axis...  13.9 us
    ppermute x10, waiting for transfers between devices, xored(): lax.ppermute(value, axis, [(i, i ^ bit) for i in range(lax.axis_size(axis...  10.1 us
    pallas_call x1, Pallas kernels, fast_inner(): pl.pallas_call(gram_body, out_shape=(pltpu.VMEM((2, side_tiles, vox), jnp...  6.83 us
    ppermute x1, starting transfers between devices, flipped(): return lax.ppermute(value, axes, [(i, size - 1 - i) for i in range(size)])  6.58 us
    all_to_all x1, waiting for transfers between devices, fast_inner(): every = lax.all_to_all(step, 'gx', 0, 0)  6.24 us
    all_to_all x1, starting transfers between devices, fast_inner(): every = lax.all_to_all(step, 'gx', 0, 0)  5.07 us
    ppermute x1, waiting for transfers between devices, flipped(): return lax.ppermute(value, axes, [(i, size - 1 - i) for i in range(size)])  3.89 us
    pallas_call x1, Pallas kernels, fast_inner(): pl.pallas_call(solve_body, out_shape=(jax.ShapeDtypeStruct((ngx, per, vox...  3.29 us
  transfers between devices with their start and end apart: 12, of which 8 were waited for; matrix products, arithmetic and copies ran while one was open for 1% of the time, Pallas kernels for 3%

profile of v5, /device:TPU:0, one launch (start us, length us, event | category | flops | bytes accessed | tf_op | source)
XLA Modules:
  0.0 61.9 jit_solution(13295098935310062608)
XLA Ops:
  0.6 0.0 copy-start.1
  0.6 0.0 copy-start
  0.7 6.8 %gram.1 = (f32[2,128,128]{2,1,0:T(8,128)S(1)}, f32[16,64,128]{2,1,0:T(8,128)S(1)}, f32[16,64,128]{2,1,0:T(8,128)S(1)}, f32[2,16,8,128]{3,2,1,0:T(8,128)S(1)}, bf16[2,128,64,128]{3,2,1,0:T(8,128)(2,1)S(1)}) custom-call(s32[256]{0:T(256)} %tb.1, bf16[2,128,64,128]{3,2,1,0:T(8,128)(2,1)} %bitcast.11, f32[64,128]{1,0:T(8,128)} %bitcast.13), custom_call_target="tpu_custom_call" | custom-call | tf_op jit(solution)/shard_map/gram/pallas_call | solution.py:306
  7.5 0.6 collective-permute-start
  8.0 0.0 copy-done
  8.0 6.6 %collective-permute-start.4 = (f32[256,128]{1,0:T(8,128)S(1)}, f32[256,128]{1,0:T(8,128)S(1)}, u32[]{:S(2)}, u32[]{:S(2)}) collective-permute-start(f32[256,128]{1,0:T(8,128)S(1)} %copy-done), channel_id=1, source_target_pairs={{0,31},{1,30},{2,29},{3,28},{4,27},{5,26},{6,25},{7,24},{8,23},{9,... | collective-permute-start | bytes 393224 | tf_op jit(solution)/shard_map/ppermute | solution.py:20
  14.6 3.9 %collective-permute-done.4 = f32[256,128]{1,0:T(8,128)S(1)} collective-permute-done((f32[256,128]{1,0:T(8,128)S(1)}, f32[256,128]{1,0:T(8,128)S(1)}, u32[]{:S(2)}, u32[]{:S(2)}) %collective-permute-start.4) | collective-permute-done | bytes 131104 | tf_op jit(solution)/shard_map/ppermute | solution.py:20
  18.5 0.0 copy-done.1
  18.5 1.6 %grad.1 = (f32[16,8,128]{2,1,0:T(8,128)S(1)}, f32[16,8,128]{2,1,0:T(8,128)S(1)}) custom-call(s32[1,256]{1,0:T(1,128)S(1)} %bitcast.10, bf16[2,128,64,128]{3,2,1,0:T(8,128)(2,1)S(1)} %get-tuple-element.13.jbuf, f32[2,128,128]{2,1,0:T(8,128)S(1)} %get-tuple-element.14.calc_ref, f32[2,128,128]{2,1,0:T(8,128)S(1)} %bitcast.8, f32[2,128,128]{2,1,0:T(8,128)S(1)} %bitcast.9, ...), custom_call_target="tpu_custom_call" | custom-call | tf_op jit(solution)/shard_map/grad/pallas_call | solution.py:327
  20.1 0.2 collective-permute-start.5
  20.2 1.2 %collective-permute-done.5 = f32[16,8,128]{2,1,0:T(8,128)S(1)} collective-permute-done((f32[16,8,128]{2,1,0:T(8,128)S(1)}, f32[16,8,128]{2,1,0:T(8,128)S(1)}, u32[]{:S(2)}, u32[]{:S(2)}) %collective-permute-start.5) | collective-permute-done | bytes 65568 | tf_op jit(solution)/shard_map/ppermute | solution.py:24
  21.4 1.1 %collective-permute-start.6 = (f32[4,8,128]{2,1,0:T(8,128)S(1)}, f32[4,8,128]{2,1,0:T(8,128)S(1)}, u32[]{:S(2)}, u32[]{:S(2)}) collective-permute-start(f32[4,8,128]{2,1,0:T(8,128)S(1)} %get-tuple-element.25), channel_id=1, source_target_pairs={{0,2},{2,0},{4,6},{6,4},{8,10},{10,8},{12,14},{14,12},{16,18},{18,... | collective-permute-start | bytes 49160 | tf_op jit(solution)/shard_map/ppermute | solution.py:24
  22.5 1.5 %collective-permute-start.7 = (f32[4,8,128]{2,1,0:T(8,128)S(1)}, f32[4,8,128]{2,1,0:T(8,128)S(1)}, u32[]{:S(2)}, u32[]{:S(2)}) collective-permute-start(f32[4,8,128]{2,1,0:T(8,128)S(1)} %get-tuple-element.27), channel_id=1, source_target_pairs={{0,4},{2,6},{4,0},{6,2},{8,12},{10,14},{12,8},{14,10},{16,20},{18,... | collective-permute-start | bytes 49160 | tf_op jit(solution)/shard_map/ppermute | solution.py:24
  24.1 0.9 %collective-permute-start.8 = (f32[4,8,128]{2,1,0:T(8,128)S(1)}, f32[4,8,128]{2,1,0:T(8,128)S(1)}, u32[]{:S(2)}, u32[]{:S(2)}) collective-permute-start(f32[4,8,128]{2,1,0:T(8,128)S(1)} %get-tuple-element.26), channel_id=1, source_target_pairs={{0,6},{2,4},{4,2},{6,0},{8,14},{10,12},{12,10},{14,8},{16,22},{18,... | collective-permute-start | bytes 49160 | tf_op jit(solution)/shard_map/ppermute | solution.py:24
  25.0 0.0 collective-permute-done
  25.0 0.1 add.27
  25.1 1.1 %collective-permute-start.1 = (f32[4,64,128]{2,1,0:T(8,128)S(1)}, f32[4,64,128]{2,1,0:T(8,128)S(1)}, u32[]{:S(2)}, u32[]{:S(2)}) collective-permute-start(f32[4,64,128]{2,1,0:T(8,128)S(1)} %get-tuple-element.20), channel_id=1, source_target_pairs={{0,2},{2,0},{4,6},{6,4},{8,10},{10,8},{12,14},{14,12},{16,18},{18,... | collective-permute-start | bytes 393224 | tf_op jit(solution)/shard_map/ppermute | solution.py:24
  26.2 1.5 %collective-permute-start.2 = (f32[4,64,128]{2,1,0:T(8,128)S(1)}, f32[4,64,128]{2,1,0:T(8,128)S(1)}, u32[]{:S(2)}, u32[]{:S(2)}) collective-permute-start(f32[4,64,128]{2,1,0:T(8,128)S(1)} %get-tuple-element.22), channel_id=1, source_target_pairs={{0,4},{2,6},{4,0},{6,2},{8,12},{10,14},{12,8},{14,10},{16,20},{18,... | collective-permute-start | bytes 393224 | tf_op jit(solution)/shard_map/ppermute | solution.py:24
  27.7 0.0 collective-permute-done.6
  27.7 0.9 %collective-permute-start.3 = (f32[4,64,128]{2,1,0:T(8,128)S(1)}, f32[4,64,128]{2,1,0:T(8,128)S(1)}, u32[]{:S(2)}, u32[]{:S(2)}) collective-permute-start(f32[4,64,128]{2,1,0:T(8,128)S(1)} %get-tuple-element.21), channel_id=1, source_target_pairs={{0,6},{2,4},{4,2},{6,0},{8,14},{10,12},{12,10},{14,8},{16,22},{18,... | collective-permute-start | bytes 393224 | tf_op jit(solution)/shard_map/ppermute | solution.py:24
  28.6 0.0 collective-permute-done.7
  28.6 0.2 collective-permute-done.8
  28.9 2.1 %collective-permute-done.1 = f32[4,64,128]{2,1,0:T(8,128)S(1)} collective-permute-done((f32[4,64,128]{2,1,0:T(8,128)S(1)}, f32[4,64,128]{2,1,0:T(8,128)S(1)}, u32[]{:S(2)}, u32[]{:S(2)}) %collective-permute-start.1) | collective-permute-done | bytes 131104 | tf_op jit(solution)/shard_map/ppermute | solution.py:24
  31.0 3.0 %collective-permute-done.2 = f32[4,64,128]{2,1,0:T(8,128)S(1)} collective-permute-done((f32[4,64,128]{2,1,0:T(8,128)S(1)}, f32[4,64,128]{2,1,0:T(8,128)S(1)}, u32[]{:S(2)}, u32[]{:S(2)}) %collective-permute-start.2) | collective-permute-done | bytes 131104 | tf_op jit(solution)/shard_map/ppermute | solution.py:24
  34.0 0.0 collective-permute-done.3
  34.0 2.5 %collective-permute-start.9 = (f32[2,72,128]{2,1,0:T(8,128)S(1)}, f32[2,72,128]{2,1,0:T(8,128)S(1)}, u32[]{:S(2)}, u32[]{:S(2)}) collective-permute-start(f32[2,72,128]{2,1,0:T(8,128)S(1)} %pad_maximum_fusion), channel_id=1, source_target_pairs={{0,8},{2,10},{4,12},{6,14},{8,0},{10,2},{12,4},{14,6},{16,24},{18,... | collective-permute-start | bytes 221192 | tf_op jit(solution)/shard_map/ppermute | solution.py:24
  36.6 2.3 %collective-permute-done.9 = f32[2,72,128]{2,1,0:T(8,128)S(1)} collective-permute-done((f32[2,72,128]{2,1,0:T(8,128)S(1)}, f32[2,72,128]{2,1,0:T(8,128)S(1)}, u32[]{:S(2)}, u32[]{:S(2)}) %collective-permute-start.9) | collective-permute-done | bytes 73760 | tf_op jit(solution)/shard_map/ppermute | solution.py:24
  38.9 3.5 %collective-permute-start.10 = (f32[1,72,128]{2,1,0:T(8,128)S(1)}, f32[1,72,128]{2,1,0:T(8,128)S(1)}, u32[]{:S(2)}, u32[]{:S(2)}) collective-permute-start(f32[1,72,128]{2,1,0:T(8,128)S(1)} %get-tuple-element.23), channel_id=1, source_target_pairs={{0,16},{2,18},{4,20},{6,22},{8,24},{10,26},{12,28},{14,30},{16,0},... | collective-permute-start | bytes 110600 | tf_op jit(solution)/shard_map/ppermute | solution.py:24
  43.1 1.3 %collective-permute-done.10.b_ref = f32[1,72,128]{2,1,0:T(8,128)S(1)} collective-permute-done((f32[1,72,128]{2,1,0:T(8,128)S(1)}, f32[1,72,128]{2,1,0:T(8,128)S(1)}, u32[]{:S(2)}, u32[]{:S(2)}) %collective-permute-start.10) | collective-permute-done | bytes 36896 | tf_op jit(solution)/shard_map/ppermute | solution.py:24
  44.4 3.3 %solve.1 = (f32[16,4,128]{2,1,0:T(4,128)}, f32[8,128]{1,0:T(8,128)S(1)}) custom-call(f32[1]{0:T(128)S(6)} %copy.8.damp, f32[1,72,128]{2,1,0:T(8,128)S(1)} %get-tuple-element.24.a_ref, f32[1,72,128]{2,1,0:T(8,128)S(1)} %collective-permute-done.10.b_ref), custom_call_target="tpu_custom_call" | custom-call | tf_op jit(solution)/shard_map/solve/pallas_call | solution.py:349
  47.7 5.1 %all-to-all-start = ((f32[16,4,128]{2,1,0:T(4,128)}), f32[16,4,128]{2,1,0:T(4,128)S(1)}, u32[]{:S(2)}, u32[]{:S(2)}) async-start(f32[16,4,128]{2,1,0:T(4,128)} %get-tuple-element.18), calls=%async_computation | async-start | bytes 65536 | tf_op jit(solution)/shard_map/all_to_all | solution.py:357
  52.7 0.5 slice.63
  53.9 6.2 %all-to-all-done = f32[16,4,128]{2,1,0:T(4,128)S(1)} async-done(((f32[16,4,128]{2,1,0:T(4,128)}), f32[16,4,128]{2,1,0:T(4,128)S(1)}, u32[]{:S(2)}, u32[]{:S(2)}) %all-to-all-start) | async-done | bytes 32800 | tf_op jit(solution)/shard_map/all_to_all | solution.py:357
  60.1 0.6 copy.9
  (8 shorter events, 0.1 us)
Async XLA Ops:
  0.6 17.9 %copy-start.1 = (s32[256]{0:T(256)S(1)}, s32[256]{0:T(256)}, u32[]{:S(2)}) copy-start(s32[256]{0:T(256)} %tb.1) | copy-start | bytes 3076
  0.6 7.4 %copy-start = (f32[256,128]{1,0:T(8,128)S(1)}, f32[256,128]{1,0:T(8,128)}, u32[]{:S(2)}) copy-start(f32[256,128]{1,0:T(8,128)} %param.5) | copy-start | bytes 393220
  7.5 17.5 %collective-permute-start = (f32[16,64,128]{2,1,0:T(8,128)S(1)}, f32[16,64,128]{2,1,0:T(8,128)S(1)}, u32[]{:S(2)}, u32[]{:S(2)}) collective-permute-start(f32[16,64,128]{2,1,0:T(8,128)S(1)} %get-tuple-element.12), channel_id=1, source_target_pairs={{0,1},{1,0},{2,3},{3,2},{4,5},{5,4},{6,7},{7,6},{8,9},{9,8},{10,11... | collective-permute-start | bytes 1572872 | tf_op jit(solution)/shard_map/ppermute | solution.py:24
  8.0 10.5 %collective-permute-start.4 = (f32[256,128]{1,0:T(8,128)S(1)}, f32[256,128]{1,0:T(8,128)S(1)}, u32[]{:S(2)}, u32[]{:S(2)}) collective-permute-start(f32[256,128]{1,0:T(8,128)S(1)} %copy-done), channel_id=1, source_target_pairs={{0,31},{1,30},{2,29},{3,28},{4,27},{5,26},{6,25},{7,24},{8,23},{9,... | collective-permute-start | bytes 393224 | tf_op jit(solution)/shard_map/ppermute | solution.py:20
  20.1 1.3 %collective-permute-start.5 = (f32[16,8,128]{2,1,0:T(8,128)S(1)}, f32[16,8,128]{2,1,0:T(8,128)S(1)}, u32[]{:S(2)}, u32[]{:S(2)}) collective-permute-start(f32[16,8,128]{2,1,0:T(8,128)S(1)} %get-tuple-element.17), channel_id=1, source_target_pairs={{0,1},{1,0},{2,3},{3,2},{4,5},{5,4},{6,7},{7,6},{8,9},{9,8},{10,11... | collective-permute-start | bytes 196616 | tf_op jit(solution)/shard_map/ppermute | solution.py:24
  21.4 6.3 %collective-permute-start.6 = (f32[4,8,128]{2,1,0:T(8,128)S(1)}, f32[4,8,128]{2,1,0:T(8,128)S(1)}, u32[]{:S(2)}, u32[]{:S(2)}) collective-permute-start(f32[4,8,128]{2,1,0:T(8,128)S(1)} %get-tuple-element.25), channel_id=1, source_target_pairs={{0,2},{2,0},{4,6},{6,4},{8,10},{10,8},{12,14},{14,12},{16,18},{18,... | collective-permute-start | bytes 49160 | tf_op jit(solution)/shard_map/ppermute | solution.py:24
  22.5 6.1 %collective-permute-start.7 = (f32[4,8,128]{2,1,0:T(8,128)S(1)}, f32[4,8,128]{2,1,0:T(8,128)S(1)}, u32[]{:S(2)}, u32[]{:S(2)}) collective-permute-start(f32[4,8,128]{2,1,0:T(8,128)S(1)} %get-tuple-element.27), channel_id=1, source_target_pairs={{0,4},{2,6},{4,0},{6,2},{8,12},{10,14},{12,8},{14,10},{16,20},{18,... | collective-permute-start | bytes 49160 | tf_op jit(solution)/shard_map/ppermute | solution.py:24
  24.1 4.8 %collective-permute-start.8 = (f32[4,8,128]{2,1,0:T(8,128)S(1)}, f32[4,8,128]{2,1,0:T(8,128)S(1)}, u32[]{:S(2)}, u32[]{:S(2)}) collective-permute-start(f32[4,8,128]{2,1,0:T(8,128)S(1)} %get-tuple-element.26), channel_id=1, source_target_pairs={{0,6},{2,4},{4,2},{6,0},{8,14},{10,12},{12,10},{14,8},{16,22},{18,... | collective-permute-start | bytes 49160 | tf_op jit(solution)/shard_map/ppermute | solution.py:24
  25.1 5.9 %collective-permute-start.1 = (f32[4,64,128]{2,1,0:T(8,128)S(1)}, f32[4,64,128]{2,1,0:T(8,128)S(1)}, u32[]{:S(2)}, u32[]{:S(2)}) collective-permute-start(f32[4,64,128]{2,1,0:T(8,128)S(1)} %get-tuple-element.20), channel_id=1, source_target_pairs={{0,2},{2,0},{4,6},{6,4},{8,10},{10,8},{12,14},{14,12},{16,18},{18,... | collective-permute-start | bytes 393224 | tf_op jit(solution)/shard_map/ppermute | solution.py:24
  26.2 7.8 %collective-permute-start.2 = (f32[4,64,128]{2,1,0:T(8,128)S(1)}, f32[4,64,128]{2,1,0:T(8,128)S(1)}, u32[]{:S(2)}, u32[]{:S(2)}) collective-permute-start(f32[4,64,128]{2,1,0:T(8,128)S(1)} %get-tuple-element.22), channel_id=1, source_target_pairs={{0,4},{2,6},{4,0},{6,2},{8,12},{10,14},{12,8},{14,10},{16,20},{18,... | collective-permute-start | bytes 393224 | tf_op jit(solution)/shard_map/ppermute | solution.py:24
  27.7 6.3 %collective-permute-start.3 = (f32[4,64,128]{2,1,0:T(8,128)S(1)}, f32[4,64,128]{2,1,0:T(8,128)S(1)}, u32[]{:S(2)}, u32[]{:S(2)}) collective-permute-start(f32[4,64,128]{2,1,0:T(8,128)S(1)} %get-tuple-element.21), channel_id=1, source_target_pairs={{0,6},{2,4},{4,2},{6,0},{8,14},{10,12},{12,10},{14,8},{16,22},{18,... | collective-permute-start | bytes 393224 | tf_op jit(solution)/shard_map/ppermute | solution.py:24
  34.0 4.9 %collective-permute-start.9 = (f32[2,72,128]{2,1,0:T(8,128)S(1)}, f32[2,72,128]{2,1,0:T(8,128)S(1)}, u32[]{:S(2)}, u32[]{:S(2)}) collective-permute-start(f32[2,72,128]{2,1,0:T(8,128)S(1)} %pad_maximum_fusion), channel_id=1, source_target_pairs={{0,8},{2,10},{4,12},{6,14},{8,0},{10,2},{12,4},{14,6},{16,24},{18,... | collective-permute-start | bytes 221192 | tf_op jit(solution)/shard_map/ppermute | solution.py:24
  38.9 5.4 %collective-permute-start.10 = (f32[1,72,128]{2,1,0:T(8,128)S(1)}, f32[1,72,128]{2,1,0:T(8,128)S(1)}, u32[]{:S(2)}, u32[]{:S(2)}) collective-permute-start(f32[1,72,128]{2,1,0:T(8,128)S(1)} %get-tuple-element.23), channel_id=1, source_target_pairs={{0,16},{2,18},{4,20},{6,22},{8,24},{10,26},{12,28},{14,30},{16,0},... | collective-permute-start | bytes 110600 | tf_op jit(solution)/shard_map/ppermute | solution.py:24
  47.7 12.5 %all-to-all-start = ((f32[16,4,128]{2,1,0:T(4,128)}), f32[16,4,128]{2,1,0:T(4,128)S(1)}, u32[]{:S(2)}, u32[]{:S(2)}) async-start(f32[16,4,128]{2,1,0:T(4,128)} %get-tuple-element.18), calls=%async_computation | async-start | bytes 65536 | tf_op jit(solution)/shard_map/all_to_all | solution.py:357
